TPU v7x, 128 devices: a whole 4x4x4 slice. The times are simulated.
128 devices in a mesh: tm: 16 (over x, y), space: 8 (over z, core).
Axes of the slice: x: 4, y: 4, z: 4, core: 2. Of those that a mesh axis runs over, the one named last changes fastest.
Arguments:
- frames: bfloat16 [8192, 8, 256], P('tm', 'space'), may hold values from -8 to 8
- patch_cell: int32 [8], P('space'), may hold values from 0 to 2047
- enc_in: bfloat16 [256, 1024], replicated, may hold values from -0.375 to 0.375
- enc_bias: float32 [1024], replicated, may hold values from -3 to 3
- enc_out: bfloat16 [1024, 1024], replicated, may hold values from -0.1875 to 0.1875
- pos_table: bfloat16 [2048, 1024], replicated, may hold values from -3 to 3
- norm_gain: float32 [1024], replicated, may hold values from 0.1 to 1.9
- w_pair: bfloat16 [1024, 4096], replicated, may hold values from -0.1875 to 0.1875
- w_keys: bfloat16 [1024, 256], replicated, may hold values from -0.0234375 to 0.0234375
- w_step: bfloat16 [1024, 32], replicated, may hold values from -0.1875 to 0.1875
- step_bias: float32 [32], replicated, may hold values from -1.5 to 1
- decay_code: int32 [32], replicated, may hold values from 0 to 15
- skip_gain: float32 [32], replicated, may hold values from 0.5 to 1.5
- out_gain: float32 [2048], replicated, may hold values from 0.1 to 1.9
- w_out: bfloat16 [2048, 1024], replicated, may hold values from -0.125 to 0.125
Outputs:
- layer_output: bfloat16 [8192, 8, 1024], P('tm', 'space')
All inputs are finite; a program needn't handle non-finite values.
Results may differ from a plain program's by a relative error of at most 0.013.
Values may be sent and summed in bfloat16 or wider, within the bound.
A program may use at most 128 MiB of HBM per device.

v0:
```python
import jax
import jax.numpy as jnp
from jax import lax
from jax.sharding import PartitionSpec as P


def carried_in(array, axis, combine, identity):
    peers, here = (lax.axis_size(axis), lax.axis_index(axis))
    everything = jax.tree.map(lambda part: lax.all_gather(part, axis), array)
    start = jax.tree.map(
        lambda part, zero: jnp.broadcast_to(jnp.asarray(zero, part.dtype), part.shape),
        array,
        identity,
    )

    def turn(k, before):
        reached = k < here
        new = combine(before, jax.tree.map(lambda part: part[k], everything))
        return jax.tree.map(lambda a, b: jnp.where(reached, a, b), new, before)

    return lax.fori_loop(0, peers, turn, start)


def rate_table(decay_code):
    return -0.0005 - 0.003 * decay_code.astype(jnp.float32)


def encode(frame_block, pos_rows, enc_in, enc_bias, enc_out, norm_gain):
    hidden = jax.nn.gelu(
        jnp.dot(frame_block, enc_in, preferred_element_type=jnp.float32) + enc_bias,
        approximate=True,
    ).astype(jnp.bfloat16)
    encoded = (
        jnp.dot(hidden, enc_out, preferred_element_type=jnp.float32) + pos_rows.astype(jnp.float32)
    ).astype(jnp.bfloat16)
    widened = encoded.astype(jnp.float32)
    normed = (
        widened * lax.rsqrt(jnp.mean(widened * widened, axis=-1, keepdims=True) + 1e-05) * norm_gain
    ).astype(jnp.bfloat16)
    return (encoded, normed)


def body(
    frames,
    patch_cell,
    enc_in,
    enc_bias,
    enc_out,
    pos_table,
    norm_gain,
    w_pair,
    w_keys,
    w_step,
    step_bias,
    decay_code,
    skip_gain,
    out_gain,
    w_out,
):
    frame_count = frames.shape[0]
    own_count = frames.shape[1]
    heads_all = w_step.shape[1]
    head_dim = w_pair.shape[1] // (2 * heads_all)
    spread = lax.axis_size("space")
    local_heads = heads_all // spread
    head_start = lax.axis_index("space") * local_heads
    pos_rows = jnp.take(pos_table, patch_cell, axis=0)
    decay_rates = lax.dynamic_slice_in_dim(rate_table(decay_code), head_start, local_heads)
    skip_row = lax.dynamic_slice_in_dim(skip_gain, head_start, local_heads)
    gain_rows = lax.dynamic_slice_in_dim(
        out_gain, head_start * head_dim, local_heads * head_dim
    ).reshape(local_heads, head_dim)
    encoded, normed = encode(frames, pos_rows, enc_in, enc_bias, enc_out, norm_gain)
    everyone = lax.all_gather(normed, "space", axis=1, tiled=True)
    pair_weight = lax.dynamic_slice_in_dim(
        w_pair, head_start * 2 * head_dim, local_heads * 2 * head_dim, 1
    )
    step_weight = lax.dynamic_slice_in_dim(w_step, head_start, local_heads, 1)
    step_shift = lax.dynamic_slice_in_dim(step_bias, head_start, local_heads)
    pair_cols = (
        jnp.dot(everyone, pair_weight, preferred_element_type=jnp.float32)
        .astype(jnp.bfloat16)
        .reshape(frame_count, own_count * spread, local_heads, 2 * head_dim)
    )
    key_rows = jnp.dot(everyone, w_keys, preferred_element_type=jnp.float32).astype(jnp.bfloat16)
    step_sizes = jax.nn.sigmoid(
        jnp.dot(everyone, step_weight, preferred_element_type=jnp.float32) + step_shift
    ).astype(jnp.bfloat16)
    patch_total = key_rows.shape[1]
    width = key_rows.shape[2] // 2
    patch_ids = jnp.arange(patch_total, dtype=jnp.int32)

    def first_pass(patch_id):
        pair_one = lax.dynamic_index_in_dim(pair_cols, patch_id, 1, keepdims=False)
        step_one = lax.dynamic_index_in_dim(step_sizes, patch_id, 1, keepdims=False)
        key_one = lax.dynamic_index_in_dim(key_rows, patch_id, 1, keepdims=False)
        x_vals = pair_one[..., :head_dim]
        b_rows = key_one[:, :width]
        c_rows = key_one[:, width:]
        cumlog = jnp.cumsum(step_one.astype(jnp.float32) * decay_rates[None, :], axis=0)
        scores = jnp.dot(c_rows, b_rows.T, preferred_element_type=jnp.float32)
        causal = lax.broadcasted_iota(
            jnp.int32, (frame_count, frame_count), 0
        ) >= lax.broadcasted_iota(jnp.int32, (frame_count, frame_count), 1)
        log_gap = cumlog.T[:, :, None] - cumlog.T[:, None, :]
        weights = (
            jnp.where(causal[None], jnp.exp(jnp.where(causal[None], log_gap, 0.0)), 0.0)
            * scores[None]
        ).astype(jnp.bfloat16)
        inner_part = jnp.einsum("hts,shd->thd", weights, x_vals, preferred_element_type=jnp.float32)
        to_end = jnp.exp(cumlog[-1][None, :] - cumlog)
        decayed_keys = (to_end[:, :, None] * b_rows.astype(jnp.float32)[:, None, :]).astype(
            jnp.bfloat16
        )
        block_state = jnp.einsum(
            "shn,shd->hnd", decayed_keys, x_vals, preferred_element_type=jnp.float32
        )
        return (inner_part, block_state, jnp.exp(cumlog[-1]), cumlog)

    inner_parts, block_states, decay_totals, cumlogs = lax.map(first_pass, patch_ids)

    def combine(earlier, later_part):
        return (
            earlier[0] * later_part[1][:, :, None, None] + later_part[0],
            earlier[1] * later_part[1],
        )

    states_in, _ = carried_in(
        (block_states, decay_totals),
        "tm",
        combine,
        (jnp.zeros_like(block_states), jnp.ones_like(decay_totals)),
    )

    def second_pass(packed):
        patch_id, inner_part, cumlog, state_in = packed
        pair_one = lax.dynamic_index_in_dim(pair_cols, patch_id, 1, keepdims=False)
        key_one = lax.dynamic_index_in_dim(key_rows, patch_id, 1, keepdims=False)
        x_vals = pair_one[..., :head_dim]
        z_vals = pair_one[..., head_dim:]
        c_rows = key_one[:, width:]
        carried = jnp.exp(cumlog)[:, :, None] * jnp.einsum(
            "tn,hnd->thd", c_rows.astype(jnp.float32), state_in, precision=lax.Precision.HIGHEST
        )
        summed = inner_part + carried + skip_row[None, :, None] * x_vals.astype(jnp.float32)
        gated = summed * jax.nn.silu(z_vals.astype(jnp.float32))
        scaled = (
            gated
            * lax.rsqrt(jnp.mean(gated * gated, axis=-1, keepdims=True) + 1e-05)
            * gain_rows[None]
        )
        return scaled.astype(jnp.bfloat16).reshape(frame_count, local_heads * head_dim)

    outputs = lax.map(second_pass, (patch_ids, inner_parts, cumlogs, states_in))
    merged = jnp.dot(
        lax.all_to_all(outputs, "space", split_axis=0, concat_axis=2, tiled=True),
        w_out,
        preferred_element_type=jnp.float32,
    )
    return (encoded.astype(jnp.float32) + jnp.swapaxes(merged, 0, 1)).astype(jnp.bfloat16)


def solution(mesh):
    placed = (
        P("tm", "space", None),
        P("space"),
        P(),
        P(),
        P(),
        P(),
        P(),
        P(),
        P(),
        P(),
        P(),
        P(),
        P(),
        P(),
        P(),
    )
    return jax.shard_map(
        body, mesh=mesh, in_specs=placed, out_specs=P("tm", "space", None), check_vma=False
    )
```

profile of v0, /device:TPU:0, one launch (start us, length us, event | category | flops | bytes accessed | tf_op | source)
XLA Modules:
  0.0 504.7 jit_solution(2649593888520965772)
XLA Ops:
  8.1 3.0 fusion.40
  11.2 1.4 fusion.42
  12.9 52.2 %all-gather.7.cloned.1.call-done = bf16[512,8192]{1,0:T(8,128)(2,1)} async-done(((bf16[512,1024]{1,0:T(8,128)(2,1)}), bf16[512,8192]{1,0:T(8,128)(2,1)}) %all-gather.7.cloned.1.call-update) | async-done | bytes 8388624 | tf_op jit(solution)/shard_map/all_gather | solution.py:74
  65.1 16.3 %copy.69 = bf16[64,8,8,1024]{3,2,1,0:T(8,128)(2,1)} copy(bf16[64,8,8,1024]{3,1,2,0:T(8,128)(2,1)} %bitcast.167) | data formatting | bytes 16777216
  81.4 22.1 %fusion.53 = f32[512,8,4]{1,2,0:T(4,128)S(1)} fusion(bf16[512,8,1024]{2,1,0:T(8,128)(2,1)} %bitcast.164, bf16[1024,32]{0,1:T(8,128)(2,1)} %param.30, s32[]{:T(128)S(6)} %select_n.72), kind=kOutput, calls=%fused_computation.83 | convolution fusion | flops 33554432 | bytes 8462340 | tf_op jit(solution)/shard_map/dot_general | solution.py:87
  104.0 7.1 %fusion.44 = bf16[512,8,256]{2,0,1:T(8,128)(2,1)} fusion(bf16[64,8,8,1024]{3,2,1,0:T(8,128)(2,1)} %bitcast.168, bf16[1024,256]{1,0:T(8,128)(2,1)S(1)} %copy-done.5), kind=kOutput, calls=%fused_computation.76 | convolution fusion | flops 2148532224 | bytes 11010048 | tf_op jit(solution)/shard_map/dot_general | solution.py:85
  111.1 10.4 %fusion.29 = bf16[512,8,512]{0,2,1:T(8,128)(2,1)} fusion(bf16[64,8,8,1024]{3,2,1,0:T(8,128)(2,1)} %bitcast.169, bf16[1024,4096]{1,0:T(8,128)(2,1)} %param.28, s32[]{:T(128)S(6)} %select_n.71), kind=kOutput, calls=%fused_computation.62 | convolution fusion | flops 4297064448 | bytes 13631492 | tf_op jit(solution)/shard_map/dot_general | solution.py:81
  121.5 84.4 %while.41 = (s32[]{:T(128)}, f32[8,512,4,64]{1,3,2,0:T(8,128)}, f32[8,4,128,64]{2,3,1,0:T(8,128)}, f32[8,4]{0,1:T(4,128)S(1)}, f32[8,512,4]{1,2,0:T(4,128)S(1)},...) while((s32[]{:T(128)}, f32[8,512,4,64]{1,3,2,0:T(8,128)}, ...), condition=%wide.region_4.5_spmd, body=%wide.region_1.0_spmd.sunk | while | flops 241244224 | bytes 6428303 | solution.py:120
  128.2 2.3 fusion.90
  138.7 2.3 fusion.90
  149.2 2.3 fusion.90
  159.8 2.3 fusion.90
  170.4 2.3 fusion.90
  180.9 2.3 fusion.90
  191.5 2.3 fusion.90
  202.0 2.4 fusion.90
  206.8 23.9 %all-gather.3 = f32[16,8,4]{1,2,0:T(4,128)S(1)} all-gather(f32[1,8,4]{1,2,0:T(4,128)S(1)} %bitcast.177), channel_id=3, replica_groups=mesh['tm'=16,'space'=8] {'tm'}, dimensions={0}, use_global_device_ids=true | all-gather | bytes 2176 | tf_op jit(solution)/shard_map/all_gather | solution.py:9
  230.7 86.6 %all-gather.9.cloned.1.call-done = f32[128,4,128,64]{2,3,1,0:T(8,128)} async-done(((f32[8,4,128,64]{2,3,1,0:T(8,128)}), f32[128,4,128,64]{2,3,1,0:T(8,128)}) %all-gather.9.cloned.1.call-update) | async-done | bytes 16777232 | tf_op jit(solution)/shard_map/all_gather | solution.py:9
  317.3 82.5 %while.43 = (s32[]{:T(128)}, f32[8,4,128,64]{3,2,1,0:T(8,128)}, s32[]{:T(128)}, f32[16,8,4]{1,2,0:T(4,128)S(1)}, f32[16,8,4,128,64]{3,4,2,1,0:T(8,128)}, /*index=5*/s32[]{:T(128)}, s32[]{:T(128)}) while((s32[]{:T(128)}, f32[8,4,128,64]{3,2,1,0:T(8,128)}, s32[]{:T(128)}, f32[16,8,4]{1,2,0:T(4,128)S(1)}, ...), condition=%wide.region_6.7_spmd.clone, body=%wide.region_5.6_spmd.clone.sunk | while | flops 1048580 | bytes 7340777 | solution.py:21
  317.3 1.3 constant_dynamic-slice_fusion.5
  319.3 1.7 fusion.95
  323.0 3.2 fusion.95
  328.2 3.2 fusion.95
  333.5 3.2 fusion.95
  338.7 3.2 fusion.95
  344.0 3.2 fusion.95
  349.2 3.2 fusion.95
  354.5 3.2 fusion.95
  359.7 3.2 fusion.95
  365.0 3.2 fusion.95
  370.3 3.2 fusion.95
  375.5 3.2 fusion.95
  380.8 3.2 fusion.95
  386.0 3.2 fusion.95
  391.3 3.2 fusion.95
  396.5 3.2 fusion.95
  399.8 2.2 copy.64
  402.0 58.5 %while.42 = (s32[]{:T(128)}, bf16[8,512,256]{1,2,0:T(8,128)(2,1)}, f32[8,512,4,64]{1,3,2,0:T(8,128)}, f32[8,512,4]{1,2,0:T(4,128)S(1)}, s32[8]{0:T(128)S(1)}, /*...) while((s32[]{:T(128)}, bf16[8,512,256]{1,2,0:T(8,128)(2,1)}, ...), condition=%wide.region_9.10_spmd, body=%wide.region_7.9_spmd.sunk | while | flops 203425792 | bytes 6090447 | solution.py:154
  407.0 1.4 multiply_reduce_fusion.2
  414.3 1.4 multiply_reduce_fusion.2
  421.6 1.4 multiply_reduce_fusion.2
  428.9 1.4 multiply_reduce_fusion.2
  436.2 1.4 multiply_reduce_fusion.2
  443.5 1.4 multiply_reduce_fusion.2
  450.8 1.4 multiply_reduce_fusion.2
  458.2 1.4 multiply_reduce_fusion.2
  460.4 31.8 %all_to_all.15 = bf16[8,512,256]{1,2,0:T(8,128)(2,1)S(1)} all-to-all(bf16[8,512,256]{1,2,0:T(8,128)(2,1)} %get-tuple-element.211), channel_id=1, replica_groups=mesh['tm'=16,'space'=8] {'space'}, dimensions={0} | all-to-all | bytes 4194304 | tf_op jit(solution)/shard_map/all_to_all | solution.py:156
  492.2 5.7 %fusion.47 = bf16[512,1,1024]{2,0,1:T(8,128)(2,1)} fusion(bf16[512,2048]{0,1:T(8,128)(2,1)S(1)} %bitcast.171, bf16[2048,1024]{1,0:T(8,128)(2,1)} %param.35, bf16[512,1024]{1,0:T(8,128)(2,1)S(1)} %copy-done.3), kind=kOutput, calls=%fused_computation.77 | convolution fusion | flops 2149056512 | bytes 8388608 | tf_op jit(solution)/shard_map/dot_general | solution.py:155
  (327 shorter events, 114.9 us)
Async XLA Ops:
  6.5 1.6 copy-start
  6.5 58.6 %all-gather.7.cloned.1.call-start = ((), (), s32[]{:S(2)}) async-start(), calls=%async_computation.1 | async-start | bytes 9437184 | tf_op jit(solution)/shard_map/all_gather | solution.py:74
  8.1 3.1 copy-start.4
  11.2 70.3 %copy-start.2 = (bf16[512,1024]{1,0:T(8,128)(2,1)}, bf16[512,1024]{1,0:T(8,128)(2,1)S(1)}, u32[]{:S(2)}) copy-start(bf16[512,1024]{1,0:T(8,128)(2,1)S(1)} %get-tuple-element.383) | copy-start | bytes 3145732
  11.2 1.5 copy-start.6
  11.2 1.6 copy-start.7
  12.6 304.7 %all-gather.9.cloned.1.call-start = ((), (), s32[]{:S(2)}) async-start(), calls=%async_computation.2 | async-start | bytes 17825792 | tf_op jit(solution)/shard_map/all_gather | solution.py:9
  81.4 22.6 %copy-start.5 = (bf16[1024,256]{1,0:T(8,128)(2,1)S(1)}, bf16[1024,256]{1,0:T(8,128)(2,1)}, u32[]{:S(2)}) copy-start(bf16[1024,256]{1,0:T(8,128)(2,1)} %param.29) | copy-start | bytes 1572868
  121.5 84.5 %copy-start.8 = (f32[32]{0:T(128)S(1)}, f32[32]{0:T(128)}, u32[]{:S(2)}) copy-start(f32[32]{0:T(128)} %param.33) | copy-start | bytes 388
  460.4 31.8 %copy-start.3 = (bf16[512,1024]{1,0:T(8,128)(2,1)S(1)}, bf16[512,1024]{1,0:T(8,128)(2,1)}, u32[]{:S(2)}) copy-start(bf16[512,1024]{1,0:T(8,128)(2,1)} %copy-done.2) | copy-start | bytes 3145732
  492.2 5.7 %copy-start.1 = (bf16[1024,1024]{1,0:T(8,128)(2,1)S(1)}, bf16[1024,1024]{1,0:T(8,128)(2,1)}, u32[]{:S(2)}) copy-start(bf16[1024,1024]{1,0:T(8,128)(2,1)} %param.25) | copy-start | bytes 6291460
Sparse Core Ops, SparseCore 0:
  12.7 52.3 all-gather.6
  206.1 111.1 all-gather.8
where the time goes:
time: 509 us; the launch traced here: 505 us
  waiting for transfers between devices  139 us (27%)
  local copies, waits for them, and re-layouts  105 us (21%)
  matrix products  81.4 us (16%)
  other arithmetic  78.1 us (15%)
  blocking collectives  55.6 us (11%)
  loops' own time  31.8 us (6%)
  between operations  14.4 us (3%)
    all_gather x1, waiting for transfers between devices, carried_in(): everything = jax.tree.map(lambda part: lax.all_gather(part, axis), array)  86.6 us
    all_gather x1, waiting for transfers between devices, body(): everyone = lax.all_gather(normed, 'space', axis=1, tiled=True)  52.2 us
    select_n x16, other arithmetic, turn(): return jax.tree.map(lambda a, b: jnp.where(reached, a, b), new, before)  50.3 us
    all_to_all x1, blocking collectives, body(): lax.all_to_all(outputs, 'space', split_axis=0, concat_axis=2, tiled=True)  31.8 us
    dynamic_slice x32, local copies, waits for them, and re-layouts, turn(): new = combine(before, jax.tree.map(lambda part: part[k], everything))  30.4 us
    all_gather x1, blocking collectives, carried_in(): everything = jax.tree.map(lambda part: lax.all_gather(part, axis), array)  23.9 us
    dot_general x1, matrix products, body(): jnp.dot(everyone, step_weight, preferred_element_type=jnp.float32)  22.1 us
    dot_general x8, matrix products, first_pass(): jnp.einsum('hts,shd->thd', weights, x_vals, preferred_element_type=jnp.fl...  18.6 us
  transfers between devices with their start and end apart: 2, of which 2 were waited for; matrix products, arithmetic and copies ran while one was open for 0% of the time, Pallas kernels for 0%

commit v1 on v0

v1 whole, which is shorter than its diff:
```python
import jax
import jax.numpy as jnp
from jax import lax
from jax.sharding import PartitionSpec as P

F32 = jnp.float32
BF16 = jnp.bfloat16


def dot(a, b):
    return jnp.dot(a, b, preferred_element_type=F32)


def body(frames, patch_cell, enc_in, enc_bias, enc_out, pos_table, norm_gain, w_pair, w_keys,
         w_step, step_bias, decay_code, skip_gain, out_gain, w_out):
    count = frames.shape[0]
    heads = w_step.shape[1]
    hd = w_pair.shape[1] // (2 * heads)
    width = w_keys.shape[1] // 2
    peers = lax.axis_size("tm")
    here = lax.axis_index("tm")
    pos_row = lax.dynamic_slice_in_dim(pos_table, patch_cell[0], 1, 0)
    hidden = jax.nn.gelu(dot(frames[:, 0], enc_in) + enc_bias, approximate=True).astype(BF16)
    encoded = (dot(hidden, enc_out) + pos_row.astype(F32)).astype(BF16)
    wide = encoded.astype(F32)
    normed = (
        wide * lax.rsqrt(jnp.mean(wide * wide, axis=-1, keepdims=True) + 1e-05) * norm_gain
    ).astype(BF16)
    pair = dot(normed, w_pair).astype(BF16).reshape(count, heads, 2, hd)
    x = pair[:, :, 0]
    gate = pair[:, :, 1]
    keys = dot(normed, w_keys).astype(BF16)
    b, c = keys[:, :width], keys[:, width:]
    step = jax.nn.sigmoid(dot(normed, w_step) + step_bias).astype(BF16)
    rate = -0.0005 - 0.003 * decay_code.astype(F32)
    causal = lax.broadcasted_iota(jnp.int32, (count, count), 0) >= lax.broadcasted_iota(
        jnp.int32, (count, count), 1
    )
    cum = dot(causal.astype(BF16), step) * rate
    scores = jnp.where(causal, dot(c, b.T), 0.0).astype(BF16)
    scaled = (x.astype(F32) * jnp.exp(-cum)[:, :, None]).astype(BF16).reshape(count, heads * hd)
    total = jnp.exp(cum[-1])
    state = dot(b.T, scaled) * jnp.repeat(total, hd)[None]
    per = heads // peers * hd
    spread = jnp.repeat(total, hd)
    high = spread.astype(BF16)
    low = (spread - high.astype(F32)).astype(BF16)
    outgoing = jnp.concatenate(
        [state.astype(BF16), jnp.broadcast_to(high, (8, heads * hd)),
         jnp.broadcast_to(low, (8, heads * hd))], axis=0
    ).reshape(width + 16, peers, per).swapaxes(0, 1)
    arrived = lax.all_to_all(outgoing, "tm", split_axis=0, concat_axis=0, tiled=True)
    decay = arrived[:, width].astype(F32) + arrived[:, width + 8].astype(F32)
    running = jnp.zeros((width, per), F32)
    entering = []
    for k in range(peers):
        entering.append(running.astype(BF16))
        running = decay[k][None] * running + arrived[k, :width].astype(F32)
    back = lax.all_to_all(jnp.stack(entering), "tm", split_axis=0, concat_axis=0, tiled=True)
    state_in = back.swapaxes(0, 1).reshape(width, heads * hd)
    linear = dot(scores, scaled) + dot(c, state_in)
    y = linear.reshape(count, heads, hd) * jnp.exp(cum)[:, :, None] + skip_gain[None, :, None] * x.astype(F32)
    g = y * jax.nn.silu(gate.astype(F32))
    mixed = (
        g * lax.rsqrt(jnp.mean(g * g, axis=-1, keepdims=True) + 1e-05)
        * out_gain.reshape(heads, hd)[None]
    ).astype(BF16).reshape(count, heads * hd)
    return (encoded.astype(F32) + dot(mixed, w_out)).astype(BF16)[:, None]


def solution(mesh):
    placed = (P("tm", "space", None), P("space")) + (P(),) * 13
    return jax.shard_map(
        body, mesh=mesh, in_specs=placed, out_specs=P("tm", "space", None), check_vma=False
    )
```

time: 509 us -> 130 us (0.26)
  waiting for transfers between devices: 139 us -> 11.6 us
  local copies, waits for them, and re-layouts: 105 us -> 41.5 us
  blocking collectives: 55.6 us -> 0 us
  other arithmetic: 78.1 us -> 27.4 us
  matrix products: 81.4 us -> 37 us
  loops' own time: 31.8 us -> 0 us
  between operations: 14.4 us -> 0.89 us
  starting transfers between devices: 0.04 us -> 10.9 us
    all_gather x2 -> x0, waiting for transfers between devices: 139 us -> none  [the longest x1 86.6 us: carried_in(): everything = jax.tree.map(lambda part: lax.all_gather(part, axis), array)]
    select_n x16 -> x0, other arithmetic: 50.3 us -> none  [turn(): return jax.tree.map(lambda a, b: jnp.where(reached, a, b), new, before)]
    dot_general x29 -> x8, matrix products: 78.4 us -> 37 us  [dot(): return jnp.dot(a, b, preferred_element_type=F32)]
    dynamic_slice x60 -> x0, local copies, waits for them, and re-layouts: 41.1 us -> none  [the longest x32 30.4 us: turn(): new = combine(before, jax.tree.map(lambda part: part[k], everything))]
    squeeze x32 -> x0, local copies, waits for them, and re-layouts: 32.9 us -> none  [the longest x8 8.66 us: second_pass(): pair_one = lax.dynamic_index_in_dim(pair_cols, patch_id, 1, keepdims=False)]
    another operation x3 -> x0, loops' own time: 31.8 us -> none  [the longest x1 15.9 us: body(): outputs = lax.map(second_pass, (patch_ids, inner_parts, cumlogs, states_in))]
    all_to_all x1 -> x0, blocking collectives: 31.8 us -> none  [body(): lax.all_to_all(outputs, 'space', split_axis=0, concat_axis=2, tiled=True)]
    all_gather x1 -> x0, blocking collectives: 23.9 us -> none  [carried_in(): everything = jax.tree.map(lambda part: lax.all_gather(part, axis), array)]
  transfers between devices with their start and end apart: 2 -> 2, of which waited for: 2 -> 1; matrix products, arithmetic and copies ran while one was open for 0% -> 18% of each run, Pallas kernels for 0% -> 0%
where the time goes in v1:
time: 130 us; the launch traced here: 129 us
  local copies, waits for them, and re-layouts  41.5 us (32%)
  matrix products  37 us (28%)
  other arithmetic  27.4 us (21%)
  waiting for transfers between devices  11.6 us (9%)
  starting transfers between devices  10.9 us (8%)
    dot_general x8, matrix products, dot(): return jnp.dot(a, b, preferred_element_type=F32)  37 us
    all_to_all x1, waiting for transfers between devices, body(): lax.all_to_all(outgoing, 'tm', split_axis=0, concat_axis=0, tiled=True)  11.6 us
    unnamed x14, other arithmetic  9.88 us
    mul x2, local copies, waits for them, and re-layouts, body(): linear.reshape(count, heads, hd) * jnp.exp(cum)[:, :, None]  7.94 us
    mul x2, local copies, waits for them, and re-layouts, body(): g * lax.rsqrt(jnp.mean(g * g, axis=-1, keepdims=True) + 1e-05)  7.88 us
    all_to_all x1, starting transfers between devices, body(): lax.all_to_all(outgoing, 'tm', split_axis=0, concat_axis=0, tiled=True)  7.14 us
    convert_element_type x1, other arithmetic, body(): g = y * jax.nn.silu(gate.astype(F32))  6.84 us
    convert_element_type x1, local copies, waits for them, and re-layouts, body(): pair = dot(normed, w_pair).astype(BF16).reshape(count, heads, 2, hd)  6.48 us
  transfers between devices with their start and end apart: 2, of which 1 were waited for; matrix products, arithmetic and copies ran while one was open for 18% of the time, Pallas kernels for 0%

profile of v1, /device:TPU:0, one launch (start us, length us, event | category | flops | bytes accessed | tf_op | source)
XLA Modules:
  0.0 129.2 jit_solution(16874755592820709412)
XLA Ops:
  0.0 0.8 multiply_subtract_fusion
  1.5 0.7 dynamic-slice_convert_fusion
  2.2 4.0 %fusion.17 = (f32[512]{0:T(512)S(1)}, bf16[512,1024]{1,0:T(8,128)(2,1)}) fusion(f32[1024]{0:T(1024)S(1)} %bitcast.112, bf16[1024,1024]{1,0:T(8,128)(2,1)S(1)} %copy-done, bf16[256,1024]{1,0:T(8,128)(2,1)} %param.17, f32[1024]{0:T(1024)} %param.18, bf16[512,1,256]{2,0,1:T(8,128)(2,1)} %param.15), kind=kOutput, calls=%fused_computation.29 | convolution fusion | flops 1350041088 | bytes 3942400 | tf_op jit(solution)/shard_map/dot_general | solution.py:11
  6.2 10.3 %convolution_convert_fusion = bf16[512,4096]{1,0:T(8,128)(2,1)} fusion(bf16[1024,4096]{1,0:T(8,128)(2,1)} %param.22, bf16[512,1024]{1,0:T(8,128)(2,1)} %get-tuple-element.52, f32[1024]{0:T(1024)S(1)} %copy-done.6, f32[512]{0:T(512)S(1)} %add_rsqrt_fusion.1), kind=kOutput, calls=%fused_computation | convolution fusion | flops 4299161600 | bytes 13637632 | tf_op jit(solution)/shard_map/dot_general | solution.py:11
  16.5 6.5 %copy.38 = bf16[512,4096]{0,1:T(8,128)(2,1)} copy(bf16[512,4096]{1,0:T(8,128)(2,1)} %convolution_convert_fusion) | data formatting | bytes 8388608 | tf_op jit(solution)/shard_map/convert_element_type | solution.py:29
  23.0 6.8 %slice_convert_fusion = (f32[512,32,1,64]{0,3,2,1:T(8,128)}, f32[512,32,1,64]{0,3,1,2:T(8,128)}) fusion(bf16[512,32,2,64]{0,3,2,1:T(8,128)(2,1)} %bitcast.105), kind=kLoop, calls=%fused_computation.33 | loop fusion | flops 2097152 | bytes 12582912 | tf_op jit(solution)/shard_map/convert_element_type | solution.py:63
  29.8 0.5 convolution_convert_fusion.1
  30.3 0.7 negate_exponential_fusion
  31.0 0.2 fusion.50
  31.4 2.8 %fusion.6 = bf16[512,2048]{0,1:T(8,128)(2,1)S(1)} fusion(f32[512,32]{0,1:T(8,128)S(1)} %get-tuple-element.34, f32[512,32,1,64]{0,3,1,2:T(8,128)} %get-tuple-element.18), kind=kLoop, calls=%fused_computation.11 | loop fusion | flops 2097152 | bytes 6356992 | tf_op jit(solution)/shard_map/convert_element_type | solution.py:41
  34.2 0.8 fusion.8
  35.0 1.0 bitcast_bitcast_fusion
  36.0 7.1 %all-to-all-start = ((bf16[16,144,128]{2,1,0:T(8,128)(2,1)}), bf16[16,144,128]{2,1,0:T(8,128)(2,1)S(1)}, u32[]{:S(2)}, u32[]{:S(2)}) async-start(bf16[16,144,128]{2,1,0:T(8,128)(2,1)} %bitcast_bitcast_fusion), calls=%async_computation | async-start | bytes 1179648 | tf_op jit(solution)/shard_map/all_to_all | solution.py:52
  43.2 0.6 constant_dynamic-update-slice_fusion.15
  43.8 11.6 %all-to-all-done = bf16[16,144,128]{2,1,0:T(8,128)(2,1)S(1)} async-done(((bf16[16,144,128]{2,1,0:T(8,128)(2,1)}), bf16[16,144,128]{2,1,0:T(8,128)(2,1)S(1)}, u32[]{:S(2)}, u32[]{:S(2)}) %all-to-all-start) | async-done | bytes 589856 | tf_op jit(solution)/shard_map/all_to_all | solution.py:52
  55.7 0.1 copy.65
  55.8 0.1 copy.66
  56.1 0.1 copy.68
  56.3 0.1 copy.70
  56.6 0.1 copy.72
  56.8 0.1 copy.74
  57.3 0.7 constant_dynamic-update-slice_fusion.14
  58.0 0.7 constant_dynamic-update-slice_fusion.13
  58.7 0.7 constant_dynamic-update-slice_fusion.12
  59.4 0.7 constant_dynamic-update-slice_fusion.11
  60.2 0.8 constant_dynamic-update-slice_fusion.10
  60.9 0.7 constant_dynamic-update-slice_fusion.9
  61.6 0.7 constant_dynamic-update-slice_fusion.8
  62.3 0.7 constant_dynamic-update-slice_fusion.7
  63.0 0.7 constant_dynamic-update-slice_fusion.6
  63.7 0.7 constant_dynamic-update-slice_fusion.5
  64.4 0.7 constant_dynamic-update-slice_fusion.4
  65.1 0.7 constant_dynamic-update-slice_fusion.3
  65.8 0.7 constant_dynamic-update-slice_fusion.2
  66.5 0.7 constant_dynamic-update-slice_fusion.1
  67.2 0.7 constant_dynamic-update-slice_fusion
  67.9 3.8 %all-to-all-start.1 = ((bf16[16,128,128]{1,2,0:T(8,128)(2,1)}), bf16[16,128,128]{1,2,0:T(8,128)(2,1)S(1)}, u32[]{:S(2)}, u32[]{:S(2)}) async-start(bf16[16,128,128]{1,2,0:T(8,128)(2,1)} %constant_dynamic-update-slice_fusion), calls=%async_computation.1 | async-start | bytes 1048576 | tf_op jit(solution)/shard_map/all_to_all | solution.py:59
  71.7 5.4 %copy.59 = f32[512,2048]{1,0:T(8,128)} copy(f32[512,2048]{0,1:T(8,128)} %bitcast.108) | data formatting | bytes 8388608 | tf_op jit(solution)/shard_map/convert_element_type | solution.py:63
  77.1 5.4 %copy.57 = f32[512,2048]{1,0:T(8,128)} copy(f32[512,2048]{0,1:T(8,128)} %bitcast.107) | data formatting | bytes 8388608 | tf_op jit(solution)/shard_map/convert_element_type | solution.py:41
  82.5 2.5 %mul.466 = f32[512,32,64]{0,2,1:T(8,128)} broadcast(f32[512,32]{0,1:T(8,128)S(1)} %get-tuple-element.35), dimensions={0,1} | broadcast | bytes 4259840 | tf_op jit(solution)/shard_map/mul | solution.py:62
  85.0 5.5 %copy.56 = f32[512,2048]{1,0:T(8,128)} copy(f32[512,2048]{0,1:T(8,128)} %bitcast.110) | data formatting | bytes 8388608 | tf_op jit(solution)/shard_map/mul | solution.py:62
  90.6 3.3 %fusion.25 = f32[512,2048]{1,0:T(8,128)} fusion(bf16[512,2048]{0,1:T(8,128)(2,1)S(1)} %fusion.6, bf16[512,256]{1,0:T(8,128)(2,1)S(1)} %convolution_convert_fusion.1), kind=kOutput, calls=%fused_computation.41 | convolution fusion | flops 1141637120 | bytes 6553600 | tf_op jit(solution)/shard_map/dot_general | solution.py:11
  93.9 4.8 %convolution_add_fusion = f32[512,2048]{1,0:T(8,128)} fusion(f32[512,2048]{1,0:T(8,128)} %fusion.25, bf16[128,2048]{0,1:T(8,128)(2,1)S(1)} %bitcast.111, bf16[512,256]{1,0:T(8,128)(2,1)S(1)} %convolution_convert_fusion.1), kind=kOutput, calls=%fused_computation.14 | convolution fusion | flops 269484032 | bytes 9043968 | tf_op jit(solution)/shard_map/dot_general | solution.py:11
  98.8 5.4 %copy.60 = f32[512,2048]{0,1:T(8,128)} copy(f32[512,2048]{1,0:T(8,128)} %convolution_add_fusion) | data formatting | bytes 8388608 | tf_op jit(solution)/shard_map/add | solution.py:61
  104.2 4.6 %fusion.7 = f32[512,32]{0,1:T(8,128)S(1)} fusion(f32[32]{0:T(128)S(1)} %copy-done.2, f32[512,32]{0,1:T(8,128)S(1)} %get-tuple-element.35, bf16[512,32,2,64]{0,3,2,1:T(8,128)(2,1)} %bitcast.106, f32[512,2048]{0,1:T(8,128)} %copy.60), kind=kLoop, calls=%fused_computation.13 | loop fusion | flops 12566528 | bytes 8519808 | tf_op jit(solution)/shard_map/reduce_sum | solution.py:65
  108.8 2.5 %mul.481 = f32[512,32,64]{0,2,1:T(8,128)} broadcast(f32[512,32]{0,1:T(8,128)S(1)} %add_rsqrt_fusion), dimensions={0,1} | broadcast | bytes 4259840 | tf_op jit(solution)/shard_map/mul | solution.py:65
  111.3 5.4 %copy.61 = f32[512,2048]{1,0:T(8,128)} copy(f32[512,2048]{0,1:T(8,128)} %bitcast.109) | data formatting | bytes 8388608 | tf_op jit(solution)/shard_map/mul | solution.py:65
  116.6 12.5 %fusion.23 = bf16[512,1,1024]{2,0,1:T(8,128)(2,1)} fusion(bf16[2048,1024]{1,0:T(8,128)(2,1)} %param.29, f32[512,2048]{1,0:T(8,128)} %copy.61, f32[512,2048]{1,0:T(8,128)} %copy.59, f32[512,2048]{1,0:T(8,128)} %copy.57, f32[512,2048]{1,0:T(8,128)} %convolution_add_fusion, f32[512,2048]{1,0:T(8,128)} %copy.56, f32[2048]{0:T(1024)S(1)} %copy-done.5, ...), kind=kOutput, calls=%fused_computation.38 | convolution fusion | flops 2160590848 | bytes 27279360 | tf_op jit(solution)/shard_map/dot_general | solution.py:11
  (40 shorter events, 1.5 us)
Async XLA Ops:
  0.0 2.2 %copy-start = (bf16[1024,1024]{1,0:T(8,128)(2,1)S(1)}, bf16[1024,1024]{1,0:T(8,128)(2,1)}, u32[]{:S(2)}) copy-start(bf16[1024,1024]{1,0:T(8,128)(2,1)} %param.19) | copy-start | bytes 6291460
  2.2 4.0 %copy-start.6 = (f32[1024]{0:T(1024)S(1)}, f32[1024]{0:T(1024)}, u32[]{:S(2)}) copy-start(f32[1024]{0:T(1024)} %param.21) | copy-start | bytes 12292
  23.0 6.9 %copy-start.3 = (bf16[1024,256]{1,0:T(8,128)(2,1)S(1)}, bf16[1024,256]{1,0:T(8,128)(2,1)}, u32[]{:S(2)}) copy-start(bf16[1024,256]{1,0:T(8,128)(2,1)} %param.23) | copy-start | bytes 1572868
  23.0 6.9 %copy-start.8 = (bf16[512,1024]{1,0:T(8,128)(2,1)S(1)}, bf16[512,1024]{1,0:T(8,128)(2,1)}, u32[]{:S(2)}) copy-start(bf16[512,1024]{1,0:T(8,128)(2,1)} %get-tuple-element.52) | copy-start | bytes 3145732
  23.0 7.4 %copy-start.4 = (bf16[1024,32]{0,1:T(8,128)(2,1)S(1)}, bf16[1024,32]{0,1:T(8,128)(2,1)}, u32[]{:S(2)}) copy-start(bf16[1024,32]{0,1:T(8,128)(2,1)} %param.24) | copy-start | bytes 196612
  23.0 7.4 %copy-start.7 = (f32[32]{0:T(128)S(1)}, f32[32]{0:T(128)}, u32[]{:S(2)}) copy-start(f32[32]{0:T(128)} %param.25) | copy-start | bytes 388
  36.0 19.3 %all-to-all-start = ((bf16[16,144,128]{2,1,0:T(8,128)(2,1)}), bf16[16,144,128]{2,1,0:T(8,128)(2,1)S(1)}, u32[]{:S(2)}, u32[]{:S(2)}) async-start(bf16[16,144,128]{2,1,0:T(8,128)(2,1)} %bitcast_bitcast_fusion), calls=%async_computation | async-start | bytes 1179648 | tf_op jit(solution)/shard_map/all_to_all | solution.py:52
  67.9 26.0 %all-to-all-start.1 = ((bf16[16,128,128]{1,2,0:T(8,128)(2,1)}), bf16[16,128,128]{1,2,0:T(8,128)(2,1)S(1)}, u32[]{:S(2)}, u32[]{:S(2)}) async-start(bf16[16,128,128]{1,2,0:T(8,128)(2,1)} %constant_dynamic-update-slice_fusion), calls=%async_computation.1 | async-start | bytes 1048576 | tf_op jit(solution)/shard_map/all_to_all | solution.py:59
  85.0 5.5 %copy-start.2 = (f32[32]{0:T(128)S(1)}, f32[32]{0:T(128)}, u32[]{:S(2)}) copy-start(f32[32]{0:T(128)} %param.27) | copy-start | bytes 388
  111.3 5.4 %copy-start.5 = (f32[2048]{0:T(1024)S(1)}, f32[2048]{0:T(1024)}, u32[]{:S(2)}) copy-start(f32[2048]{0:T(1024)} %param.28) | copy-start | bytes 24580
  116.6 12.5 %copy-start.1 = (bf16[1024,1024]{1,0:T(8,128)(2,1)S(1)}, bf16[1024,1024]{1,0:T(8,128)(2,1)}, u32[]{:S(2)}) copy-start(bf16[1024,1024]{1,0:T(8,128)(2,1)} %param.19) | copy-start | bytes 6291460

commit v2 on v1

v2 whole, which is shorter than its diff:
```python
import functools

import jax
import jax.numpy as jnp
from jax import lax
from jax.experimental import pallas as pl
from jax.experimental.pallas import tpu as pltpu
from jax.sharding import PartitionSpec as P

F32 = jnp.float32
BF16 = jnp.bfloat16
MESH = pl.DeviceIdType.MESH
GROUPS = 2
LANES = 256
PEERS = 16


def dot(a, b):
    return jnp.dot(a, b, preferred_element_type=F32)


def iota(shape, axis):
    return lax.broadcasted_iota(jnp.int32, shape, axis)


def kernel(
    frames_hbm, enc_in_hbm, enc_out_hbm, w_keys_hbm, w_step_hbm, w_pair_hbm, w_out_hbm,
    pos_ref, enc_bias_ref, norm_gain_ref, step_bias_ref, code_ref, skip_ref, out_gain_ref,
    out_hbm,
    frames, enc_in, enc_out, w_keys, w_step, w_pair, w_out,
    encoded, normed, b_t, c_rows, dec, masked, x_v, xs_v, sz_v, grow_v, y_v, acc, mixed, out_v, skip_lanes,
    end_out, end_in, s_out, s_in, e_out, e_in,
    load_sem, store_sem, end_send, end_recv, send1, recv1, send2, recv2,
):
    count, depth = encoded.shape
    heads = step_bias_ref.shape[1]
    width = c_rows.shape[1]
    lanes_all = x_v.shape[1]
    chunks = lanes_all // LANES
    per = chunks // GROUPS
    hd = lanes_all // heads
    me = lax.axis_index("tm")

    plan = [
        (frames_hbm, frames), (enc_in_hbm, enc_in), (enc_out_hbm, enc_out),
        (w_keys_hbm, w_keys), (w_step_hbm, w_step),
    ]
    loads = [
        pltpu.make_async_copy(src, dst, load_sem.at[n]) for n, (src, dst) in enumerate(plan)
    ]
    half = w_pair.shape[1] // GROUPS
    for g in range(GROUPS):
        loads.append(pltpu.make_async_copy(
            w_pair_hbm.at[:, pl.ds(g * half, half)], w_pair.at[:, pl.ds(g * half, half)],
            load_sem.at[5 + g],
        ))
    loads.append(pltpu.make_async_copy(w_out_hbm, w_out, load_sem.at[5 + GROUPS]))
    for load in loads:
        load.start()

    barrier = pltpu.get_barrier_semaphore()

    def greet(d, carry):
        pl.semaphore_signal(
            barrier, inc=1, device_id={"tm": lax.rem(me + d, PEERS)}, device_id_type=MESH
        )
        return carry

    lax.fori_loop(1, PEERS, greet, 0)

    for n in range(3):
        loads[n].wait()
    rows = 256

    def encode(r, carry):
        at = pl.ds(pl.multiple_of(r * rows, rows), rows)
        hidden = jax.nn.gelu(dot(frames[at, :], enc_in[...]) + enc_bias_ref[...], approximate=True)
        coded = (dot(hidden.astype(BF16), enc_out[...]) + pos_ref[...].astype(F32)).astype(BF16)
        encoded[at, :] = coded
        wide = coded.astype(F32)
        mean = jnp.mean(wide * wide, axis=-1, keepdims=True)
        normed[at, :] = (wide * lax.rsqrt(mean + 1e-05) * norm_gain_ref[...]).astype(BF16)
        return carry

    lax.fori_loop(0, count // rows, encode, 0)

    loads[3].wait()
    loads[4].wait()
    keys = dot(normed[...], w_keys[...]).astype(BF16)
    b_t[...] = keys[:, :width].T
    c_rows[...] = keys[:, width:]
    step = jax.nn.sigmoid(dot(normed[...], w_step[...]) + step_bias_ref[...]).astype(BF16)
    four = (iota((heads, 128), 1) % heads == iota((heads, 128), 0)).astype(BF16)
    step4 = dot(step, four).astype(BF16)
    code4 = dot(jnp.broadcast_to(code_ref[...], (8, heads)).astype(BF16), four)[:1]
    rate4 = -0.0005 - 0.003 * code4
    causal = iota((count, count), 0) >= iota((count, count), 1)
    cum = dot(causal.astype(BF16), step4) * rate4
    lane = iota((count, 128), 1)
    grown = jnp.exp(jnp.where(lane < 2 * heads, cum, -cum))
    high = grown.astype(BF16)
    low = (grown - high.astype(F32)).astype(BF16)
    dec[...] = jnp.where((lane // heads) % 2 == 0, high.astype(F32), low.astype(F32)).astype(BF16)
    end_out[...] = jnp.broadcast_to(jnp.exp(cum[count - 1 : count]), (8, 128))
    masked[...] = jnp.where(causal, dot(c_rows[...], b_t[...]), 0.0).astype(BF16)
    spread = (iota((heads, lanes_all), 1) // hd == iota((heads, lanes_all), 0)).astype(F32)
    skip_lanes[...] = jnp.dot(
        jnp.broadcast_to(skip_ref[...], (8, heads)), spread,
        preferred_element_type=F32, precision=lax.Precision.HIGHEST,
    )

    pl.semaphore_wait(barrier, PEERS - 1)

    def end_copy(d):
        peer = lax.rem(me + d, PEERS)
        return pltpu.make_async_remote_copy(
            src_ref=end_out, dst_ref=end_in.at[me], send_sem=end_send.at[d - 1],
            recv_sem=end_recv.at[d - 1], device_id={"tm": peer}, device_id_type=MESH,
        )

    def slice_copy(src, dst, send, recv, g, d):
        peer = lax.rem(me + d, PEERS)
        return pltpu.make_async_remote_copy(
            src_ref=src.at[g, peer], dst_ref=dst.at[g, me], send_sem=send.at[g, d - 1],
            recv_sem=recv.at[g, d - 1], device_id={"tm": peer}, device_id_type=MESH,
        )

    def each(do):
        def turn(d, carry):
            do(d)
            return carry

        lax.fori_loop(1, PEERS, turn, 0)

    each(lambda d: end_copy(d).start())
    end_in[pl.ds(me, 1)] = end_out[...][None]

    wide_rows = s_out.shape[3]
    many = wide_rows // LANES

    def project(i, g):
        j = g * per + i
        col = pl.multiple_of(j * 2 * LANES, 2 * LANES)
        at = pl.ds(pl.multiple_of(j * LANES, LANES), LANES)
        both = dot(normed[...], w_pair[:, pl.ds(col, 2 * LANES)]).astype(BF16).astype(F32)
        left = iota((count, 128), 1) < hd
        xs, zs = [], []
        for k in range(0, 2 * LANES, 256):
            v0, v1 = both[:, k : k + 128], both[:, k + 128 : k + 256]
            xs.append(jnp.where(left, v0, pltpu.roll(v1, hd, 1)))
            zs.append(jnp.where(left, pltpu.roll(v0, hd, 1), v1))
        x = jnp.concatenate(xs, axis=1)
        z = jnp.concatenate(zs, axis=1)
        row, lane = iota((128, 2 * LANES), 0), iota((128, 2 * LANES), 1)
        first = j * (LANES // hd)
        pick = (row % heads == first + (lane % LANES) // hd) & (row // (2 * heads) == lane // LANES)
        wide = dot(dec[...], pick.astype(F32).astype(BF16))
        grow = wide[:, :LANES]
        x_v[:, at] = x.astype(BF16)
        scaled = (x * wide[:, LANES:]).astype(BF16)
        xs_v[:, at] = scaled
        grow_v[:, at] = grow
        sz_v[:, at] = z * jax.nn.sigmoid(z)
        state = (dot(b_t[...], scaled) * grow[count - 1 : count]).astype(BF16)
        side = i // many
        inside = pl.ds(pl.multiple_of((i % many) * LANES, LANES), LANES)
        parts = PEERS * many // per
        s_out[g, pl.ds(side * parts, parts), :, inside] = state.reshape(
            parts, width // parts, LANES
        )

    def inner(i, g):
        at = pl.ds(pl.multiple_of((g * per + i) * LANES, LANES), LANES)
        cut = count // 2
        base = skip_lanes[0:1, at]
        top = dot(masked[:cut, :cut], xs_v[:cut, at])
        y_v[:cut, at] = top * grow_v[:cut, at] + base * x_v[:cut, at].astype(F32)
        low = dot(masked[cut:, :], xs_v[:, at])
        y_v[cut:, at] = low * grow_v[cut:, at] + base * x_v[cut:, at].astype(F32)

    def scan(g):
        each(lambda d: slice_copy(s_out, s_in, send1, recv1, g, d).wait_recv())
        s_in[g, pl.ds(me, 1)] = s_out[g, pl.ds(me, 1)]
        parts = PEERS * many // per
        side = me // parts
        first = (g * per + side * many) * (LANES // hd)
        pick = (
            iota((128, wide_rows), 0) == first + iota((128, wide_rows), 1) // hd
        ).astype(F32)
        ends = end_in[:, 0, :]
        decay = jnp.dot(ends, pick, preferred_element_type=F32, precision=lax.Precision.HIGHEST)
        running = jnp.zeros(s_in.shape[2:], F32)
        for k in range(PEERS):
            e_out[g, k] = running.astype(BF16)
            if k < PEERS - 1:
                running = decay[k : k + 1] * running + s_in[g, k].astype(F32)
        each(lambda d: slice_copy(e_out, e_in, send2, recv2, g, d).start())
        e_in[g, pl.ds(me, 1)] = e_out[g, pl.ds(me, 1)]

    def finish(i, g):
        at = pl.ds(pl.multiple_of((g * per + i) * LANES, LANES), LANES)
        parts = PEERS * many // per
        inside = pl.ds(pl.multiple_of((i % many) * LANES, LANES), LANES)
        state = e_in[g, pl.ds((i // many) * parts, parts), :, inside].reshape(width, LANES)
        y = y_v[:, at] + grow_v[:, at] * dot(c_rows[...], state)
        gated = y * sz_v[:, at]
        mean_of = jnp.where(
            iota((LANES, LANES), 0) // hd == iota((LANES, LANES), 1) // hd, 1.0 / hd, 0.0
        ).astype(BF16)
        mean = dot((gated * gated).astype(BF16), mean_of)
        mixed[:, at] = (gated * lax.rsqrt(mean + 1e-05) * out_gain_ref[:, at]).astype(BF16)

    def loop(do, n, g):
        def turn(i, carry):
            do(i, g)
            return carry

        lax.fori_loop(0, n, turn, 0)

    for g in range(GROUPS):
        loads[5 + g].wait()
        loop(project, per, g)
        each(lambda d: slice_copy(s_out, s_in, send1, recv1, g, d).start())
        if g == 0:
            each(lambda d: end_copy(d).wait_recv())
        else:
            scan(g - 1)
            loop(inner, per, g - 1)
    loop(inner, per, GROUPS - 1)
    scan(GROUPS - 1)
    loads[5 + GROUPS].wait()

    columns = 256
    deep = lanes_all // GROUPS
    for g in range(GROUPS):
        each(lambda d: slice_copy(e_out, e_in, send2, recv2, g, d).wait_recv())
        loop(finish, per, g)

        def merge(i, g):
            at = pl.ds(pl.multiple_of(i * columns, columns), columns)
            part = dot(mixed[:, pl.ds(g * deep, deep)], w_out[pl.ds(g * deep, deep), at])
            total = part + (encoded[:, at].astype(F32) if g == 0 else acc[:, at])
            if g < GROUPS - 1:
                acc[:, at] = total
            else:
                out_v[:, at] = total.astype(BF16)
                pltpu.make_async_copy(out_v.at[:, at], out_hbm.at[:, at], store_sem.at[i]).start()

        loop(merge, depth // columns, g)

    each(lambda d: end_copy(d).wait_send())
    for g in range(GROUPS):
        each(lambda d: slice_copy(s_out, s_in, send1, recv1, g, d).wait_send())
        each(lambda d: slice_copy(e_out, e_in, send2, recv2, g, d).wait_send())

    def stored(i, carry):
        at = pl.ds(pl.multiple_of(i * columns, columns), columns)
        pltpu.make_async_copy(out_v.at[:, at], out_hbm.at[:, at], store_sem.at[i]).wait()
        return carry

    lax.fori_loop(0, depth // columns, stored, 0)


def body(frames, patch_cell, enc_in, enc_bias, enc_out, pos_table, norm_gain, w_pair, w_keys,
         w_step, step_bias, decay_code, skip_gain, out_gain, w_out):
    count, pixels = frames.shape[0], frames.shape[2]
    depth = enc_out.shape[1]
    heads = w_step.shape[1]
    lanes = w_out.shape[0]
    width = w_keys.shape[1] // 2
    chunks = lanes // LANES
    per = chunks // GROUPS
    pos_row = lax.dynamic_slice_in_dim(pos_table, patch_cell[0], 1, 0)
    slice_rows = 16
    slice_lanes = width * per * LANES // (PEERS * slice_rows)
    comm = pltpu.VMEM((GROUPS, PEERS, slice_rows, slice_lanes), BF16)
    sems = pltpu.SemaphoreType.DMA((GROUPS, PEERS - 1))
    vm = pltpu.VMEM
    out = pl.pallas_call(
        kernel,
        out_shape=jax.ShapeDtypeStruct((count, depth), BF16),
        in_specs=[pl.BlockSpec(memory_space=pl.ANY)] * 7
        + [pl.BlockSpec(memory_space=pltpu.VMEM)] * 7,
        out_specs=pl.BlockSpec(memory_space=pl.ANY),
        scratch_shapes=[
            vm((count, pixels), BF16), vm((pixels, depth), BF16), vm((depth, depth), BF16),
            vm((depth, 2 * width), BF16), vm((depth, heads), BF16), vm((depth, 2 * lanes), BF16),
            vm((lanes, depth), BF16),
            vm((count, depth), BF16), vm((count, depth), BF16), vm((width, count), BF16),
            vm((count, width), BF16), vm((count, 128), BF16), vm((count, count), BF16),
            vm((count, lanes), BF16), vm((count, lanes), BF16), vm((count, lanes), F32),
            vm((count, lanes), F32), vm((count, lanes), F32), vm((count, depth), F32),
            vm((count, lanes), BF16), vm((count, depth), BF16), vm((8, lanes), F32),
            vm((8, 128), F32), vm((PEERS, 8, 128), F32), comm, comm, comm, comm,
            pltpu.SemaphoreType.DMA((6 + GROUPS,)), pltpu.SemaphoreType.DMA((depth // 256,)),
            pltpu.SemaphoreType.DMA((PEERS - 1,)), pltpu.SemaphoreType.DMA((PEERS - 1,)),
            sems, sems, sems, sems,
        ],
        compiler_params=pltpu.CompilerParams(
            collective_id=0, has_side_effects=True, vmem_limit_bytes=62 * 1024 * 1024
        ),
        name="layer",
    )(
        frames.reshape(count, pixels), enc_in, enc_out, w_keys, w_step, w_pair, w_out,
        pos_row, enc_bias[None], norm_gain[None], step_bias[None], decay_code[None],
        skip_gain[None], out_gain[None],
    )
    return out[:, None]


def solution(mesh):
    placed = (P("tm", "space", None), P("space")) + (P(),) * 13
    return jax.shard_map(
        body, mesh=mesh, in_specs=placed, out_specs=P("tm", "space", None), check_vma=False
    )
```

time: 130 us -> 43.5 us (0.33)
  Pallas kernels: 0 us -> 37.2 us
  matrix products: 37 us -> 0 us
  local copies, waits for them, and re-layouts: 41.5 us -> 5.26 us
  other arithmetic: 27.4 us -> 0 us
  waiting for transfers between devices: 11.6 us -> 0 us
  starting transfers between devices: 10.9 us -> 0 us
    pallas_call x0 -> x1, Pallas kernels: none -> 37.2 us  [body(): pl.pallas_call(kernel, out_shape=jax.ShapeDtypeStruct((count, depth), BF1...]
    dot_general x8 -> x0, matrix products: 37 us -> none  [dot(): return jnp.dot(a, b, preferred_element_type=F32)]
    convert_element_type x3 -> x0, local copies, waits for them, and re-layouts: 17.3 us -> none  [the longest x1 6.48 us: body(): pair = dot(normed, w_pair).astype(BF16).reshape(count, heads, 2, hd)]
    mul x7 -> x0, local copies, waits for them, and re-layouts: 16 us -> none  [the longest x2 7.94 us: body(): linear.reshape(count, heads, hd) * jnp.exp(cum)[:, :, None]]
    all_to_all x2 -> x0, waiting for transfers between devices: 11.6 us -> none  [the longest x1 11.6 us: body(): lax.all_to_all(outgoing, 'tm', split_axis=0, concat_axis=0, tiled=True)]
    all_to_all x2 -> x0, starting transfers between devices: 10.9 us -> none  [the longest x1 7.14 us: body(): lax.all_to_all(outgoing, 'tm', split_axis=0, concat_axis=0, tiled=True)]
    unnamed x14 -> x0, other arithmetic: 9.88 us -> none
    convert_element_type x3 -> x0, other arithmetic: 9.65 us -> none  [the longest x1 6.84 us: body(): g = y * jax.nn.silu(gate.astype(F32))]
  transfers between devices with their start and end apart: 2 -> 0, of which waited for: 1 -> 0; matrix products, arithmetic and copies ran while one was open for 18% -> 0% of each run, Pallas kernels for 0% -> 0%
where the time goes in v2:
time: 43.5 us; the launch traced here: 43.2 us
  Pallas kernels  37.2 us (86%)
  local copies, waits for them, and re-layouts  5.26 us (12%)
  between operations  0.67 us (2%)
    pallas_call x1, Pallas kernels, body(): pl.pallas_call(kernel, out_shape=jax.ShapeDtypeStruct((count, depth), BF1...  37.2 us
    unnamed x2, local copies, waits for them, and re-layouts  3.94 us
    dynamic_slice x1, local copies, waits for them, and re-layouts, body(): pos_row = lax.dynamic_slice_in_dim(pos_table, patch_cell[0], 1, 0)  1.32 us

profile of v2, /device:TPU:0, one launch (start us, length us, event | category | flops | bytes accessed | tf_op | source)
XLA Modules:
  0.0 43.2 jit_solution(14308349817034319862)
XLA Ops:
  0.7 1.3 %constant_dynamic-slice_fusion.pos_ref = bf16[1,1024]{1,0:T(2,128)(2,1)} fusion(bf16[2048,1024]{1,0:T(8,128)(2,1)} %param.20, s32[]{:T(128)S(6)} %select_n.3), kind=kLoop, calls=%fused_computation | loop fusion | bytes 4100 | tf_op jit(solution)/shard_map/dynamic_slice | solution.py:273
  2.0 1.7 %copy.16.w_step_hbm = bf16[1024,32]{1,0:T(8,128)(2,1)} copy(bf16[1024,32]{0,1:T(8,128)(2,1)} %param.24) | data formatting | bytes 131072 | tf_op args[9]
  3.7 37.2 %layer.1 = bf16[512,1024]{1,0:T(8,128)(2,1)} custom-call(bf16[512,256]{1,0:T(8,128)(2,1)} %bitcast.13, bf16[256,1024]{1,0:T(8,128)(2,1)} %enc_in_hbm.1, bf16[1024,1024]{1,0:T(8,128)(2,1)} %enc_out_hbm.1, bf16[1024,256]{1,0:T(8,128)(2,1)} %w_keys_hbm.1, bf16[1024,32]{1,0:T(8,128)(2,1)} %copy.16.w_step_hbm, bf16[1024,4096]{1,0:T(8,128)(2,1)} %w_pair_hbm.1, ...), custom_call_target="tpu_custom_call" | custom-call | tf_op jit(solution)/shard_map/layer/pallas_call | solution.py:279
  40.9 2.3 %copy.19 = bf16[512,1,1024]{2,0,1:T(8,128)(2,1)} copy(bf16[512,1,1024]{2,0,1:T(8,128)(2,1)} %bitcast.12) | data formatting | bytes 2097152

commit v3 on v1

v3 whole, which is shorter than its diff:
```python
import functools

import jax
import jax.numpy as jnp
from jax import lax
from jax.experimental import pallas as pl
from jax.experimental.pallas import tpu as pltpu
from jax.sharding import PartitionSpec as P

F32 = jnp.float32
BF16 = jnp.bfloat16
MESH = pl.DeviceIdType.MESH
GROUPS = 4
LANES = 256
PEERS = 16
ROWS = 128
VMEM_LIMIT = 60 * 1024 * 1024


def dot(a, b):
    return jnp.dot(a, b, preferred_element_type=F32)


def exact(a, b):
    return jnp.dot(a, b, preferred_element_type=F32, precision=lax.Precision.HIGHEST)


def iota(shape, axis):
    return lax.broadcasted_iota(jnp.int32, shape, axis)


def pipelined(first, second, blocks, third=None):
    first(0)
    for n in range(blocks):
        if n + 1 < blocks:
            first(n + 1)
        second(n)
        if third is not None and n > 0:
            third(n - 1)
    if third is not None:
        third(blocks - 1)


def kernel(
    frames_hbm, enc_in_hbm, enc_out_hbm, pos_hbm, w_keys_hbm, w_step_hbm, w_pair_hbm, w_out_hbm,
    cell_ref, enc_bias_ref, norm_gain_ref, step_bias_ref, code_ref, skip_ref, out_gain_ref,
    out_ref,
    frames, enc_in, enc_out, pos_table, w_keys, w_step, w_pair, w_out,
    hidden, raw, encoded, normed, step_w, step_v, b_t, c_rows, dec, masked,
    w_val, w_gate, x_v, xs_v, sz_v, grow_v, y_v, acc, mixed, skip_lanes,
    end_out, end_in, s_out, s_in, e_out, e_in,
    load_sem, end_send, end_recv, send1, recv1, send2, recv2,
):
    count, depth = encoded.shape
    heads = step_bias_ref.shape[1]
    width = c_rows.shape[1]
    lanes_all = x_v.shape[1]
    wide = lanes_all // GROUPS
    hd = lanes_all // heads
    me = lax.axis_index("tm")

    def pair_part(g):
        part = pl.ds(g * 2 * wide, 2 * wide)
        return (w_pair_hbm.at[:, part], w_pair.at[:, part])

    plan = [
        (frames_hbm, frames), (enc_in_hbm, enc_in), (enc_out_hbm, enc_out), (pos_hbm, pos_table),
        (w_keys_hbm, w_keys), (w_step_hbm, w_step),
    ]
    plan += [pair_part(g) for g in range(GROUPS)]
    plan.append((w_out_hbm, w_out))
    loads = [
        pltpu.make_async_copy(src, dst, load_sem.at[n]) for n, (src, dst) in enumerate(plan)
    ]
    for load in loads:
        load.start()

    barrier = pltpu.get_barrier_semaphore()

    def peer_at(d):
        return lax.rem(me + d, PEERS)

    for d in range(1, PEERS):
        pl.semaphore_signal(barrier, inc=1, device_id={"tm": peer_at(d)}, device_id_type=MESH)

    four = (iota((heads, 128), 1) % heads == iota((heads, 128), 0)).astype(F32)
    bias4 = exact(jnp.broadcast_to(step_bias_ref[...], (8, heads)), four)[:1]
    code4 = dot(jnp.broadcast_to(code_ref[...], (8, heads)).astype(BF16), four.astype(BF16))[:1]
    rate4 = -0.0005 - 0.003 * code4
    loads[0].wait()
    loads[1].wait()

    def hide(n):
        at = pl.ds(n * ROWS, ROWS)
        raw = dot(frames[at, :], enc_in[...]) + enc_bias_ref[...]
        hidden[at, :] = jax.nn.gelu(raw, approximate=True).astype(BF16)

    def draw(n):
        at = pl.ds(n * ROWS, ROWS)
        raw[at, :] = dot(hidden[at, :], enc_out[...])

    blocks = count // ROWS
    hide(0)
    hide(1)
    loads[2].wait()
    for n in range(blocks):
        draw(n)
        if n + 2 < blocks:
            hide(n + 2)

    for n in (3, 4, 5, 6):
        loads[n].wait()
    cell = cell_ref[0]
    near = pos_table[lax.div(cell, 16)].astype(F32)
    pos_row = jnp.sum(
        jnp.where(iota((16, depth), 0) == lax.rem(cell, 16), near, 0.0), axis=0, keepdims=True
    )
    step_w[...] = jnp.concatenate([w_step[...]] * (128 // heads), axis=0).T

    def pack(g):
        for k in range(g * (wide // 128), (g + 1) * (wide // 128)):
            v0 = w_pair[:, 256 * k : 256 * k + 128]
            v1 = pltpu.roll(w_pair[:, 256 * k + 128 : 256 * k + 256], hd, 1)
            left = iota((depth, 128), 1) < hd
            w_val[:, 128 * k : 128 * k + 128] = jnp.where(left, v0, v1)
            w_gate[:, 128 * k : 128 * k + 128] = jnp.where(left, v1, v0)

    def code(n):
        at = pl.ds(n * ROWS, ROWS)
        coded = (raw[at, :] + pos_row).astype(BF16)
        encoded[at, :] = coded
        plain = coded.astype(F32)
        mean = jnp.mean(plain * plain, axis=-1, keepdims=True)
        normed[at, :] = (plain * lax.rsqrt(mean + 1e-05) * norm_gain_ref[...]).astype(BF16)

    def key(n):
        at = pl.ds(n * ROWS, ROWS)
        keys = dot(normed[at, :], w_keys[...]).astype(BF16)
        b_t[:, at] = keys[:, :width].T
        c_rows[at, :] = keys[:, width:]
        step_v[at, :] = jax.nn.sigmoid(dot(normed[at, :], step_w[...]) + bias4).astype(BF16)

    pipelined(code, key, blocks)
    pack(0)

    half = count // 2
    lane = iota((half, 128), 1)
    for top, deep in ((0, half), (half, count)):
        causal = iota((half, deep), 0) + top >= iota((half, deep), 1)
        cum = dot(causal.astype(F32).astype(BF16), step_v[:deep, :]) * rate4
        high = cum.astype(BF16).astype(F32)
        mid = (cum - high).astype(BF16).astype(F32)
        low = cum - high - mid
        part = lane // heads
        dec[top : top + half, :] = jnp.where(
            part == 0, high, jnp.where(part == 1, mid, jnp.where(part == 2, low, 0.0))
        ).astype(BF16)
    end_out[...] = jnp.broadcast_to(jnp.exp(cum[half - 1 : half]), (8, 128))

    pl.semaphore_wait(barrier, PEERS - 1)

    def end_copy(d, n=None):
        return pltpu.make_async_remote_copy(
            src_ref=end_out if n is None else end_in.at[pl.ds(0, n)],
            dst_ref=end_in.at[me] if n is None else end_in.at[pl.ds(0, n)],
            send_sem=end_send, recv_sem=end_recv, device_id={"tm": peer_at(d)}, device_id_type=MESH,
        )

    def slice_copy(src, dst, send, recv, g, d):
        return pltpu.make_async_remote_copy(
            src_ref=src.at[g, peer_at(d)], dst_ref=dst.at[g, me], send_sem=send.at[g],
            recv_sem=recv.at[g], device_id={"tm": peer_at(d)}, device_id_type=MESH,
        )

    def all_copies(src, dst, send, recv, g):
        every = pl.ds(0, PEERS - 1)
        return pltpu.make_async_remote_copy(
            src_ref=src.at[g, every], dst_ref=dst.at[g, every], send_sem=send.at[g],
            recv_sem=recv.at[g], device_id={"tm": peer_at(1)}, device_id_type=MESH,
        )

    for d in range(1, PEERS):
        end_copy(d).start()
    end_in[pl.ds(me, 1)] = end_out[...][None]

    sides = wide // LANES
    parts = PEERS // sides
    rows = width // parts

    def values(g):
        if g + 1 < GROUPS:
            loads[7 + g].wait()
        at = pl.ds(g * wide, wide)
        x = dot(normed[...], w_val[:, at]).astype(BF16)
        x_v[:, at] = x
        row, lane = iota((128, wide), 0), iota((128, wide), 1)
        pick = (row % heads == g * (wide // hd) + lane // hd) & (row < 3 * heads)
        cum = dot(dec[...], pick.astype(F32).astype(BF16))
        grow = jnp.exp(cum)
        grow_v[:, at] = grow
        scaled = (x.astype(F32) * jnp.exp(-cum)).astype(BF16)
        xs_v[:, at] = scaled
        state = (dot(b_t[...], scaled) * grow[count - 1 : count]).astype(BF16)
        for side in range(sides):
            s_out[g, pl.ds(side * parts, parts)] = state[
                :, side * LANES : (side + 1) * LANES
            ].reshape(parts, rows, LANES)
        if g + 1 < GROUPS:
            pack(g + 1)
        for d in range(1, PEERS):
            slice_copy(s_out, s_in, send1, recv1, g, d).start()

    def gates(g):
        at = pl.ds(g * wide, wide)
        z = dot(normed[...], w_gate[:, at]).astype(BF16).astype(F32)
        z = z * jax.nn.sigmoid(z)
        for k in range(wide // 128):
            sz_v[:, pl.ds(g * wide + 128 * k, 128)] = pltpu.roll(z[:, 128 * k : 128 * k + 128], hd, 1)

    def inner(g):
        at = pl.ds(g * wide, wide)
        base = skip_lanes[0:1, at]
        for top, deep in ((0, half), (half, count)):
            here = pl.ds(top, half)
            sums = dot(masked[here, :deep], xs_v[:deep, at])
            y_v[here, at] = sums * grow_v[here, at] + base * x_v[here, at].astype(F32)

    def scan(g):
        first = (g * sides + me // parts) * (LANES // hd)
        pick = (iota((128, LANES), 0) == first + iota((128, LANES), 1) // hd).astype(F32)
        decay = exact(end_in[:, 0, :], pick)
        all_copies(s_out, s_in, send1, recv1, g).wait_recv()
        s_in[g, pl.ds(me, 1)] = s_out[g, pl.ds(me, 1)]
        running = jnp.zeros(s_in.shape[2:], F32)
        for k in range(PEERS):
            e_out[g, k] = running.astype(BF16)
            if k < PEERS - 1:
                running = decay[k : k + 1] * running + s_in[g, k].astype(F32)
        for d in range(1, PEERS):
            slice_copy(e_out, e_in, send2, recv2, g, d).start()
        e_in[g, pl.ds(me, 1)] = e_out[g, pl.ds(me, 1)]

    mean_of = jnp.where(
        iota((LANES, LANES), 0) // hd == iota((LANES, LANES), 1) // hd, 1.0 / hd, 0.0
    ).astype(BF16)

    def finish(g, n):
        here = pl.ds(n * ROWS, ROWS)
        for side in range(sides):
            at = pl.ds(g * wide + side * LANES, LANES)
            state = e_in[g, pl.ds(side * parts, parts)].reshape(width, LANES)
            y = y_v[here, at] + grow_v[here, at] * dot(c_rows[here, :], state)
            gated = y * sz_v[here, at]
            mean = dot((gated * gated).astype(BF16), mean_of)
            mixed[here, at] = (gated * lax.rsqrt(mean + 1e-05) * out_gain_ref[:, at]).astype(BF16)

    def merge(g, n):
        here = pl.ds(n * ROWS, ROWS)
        at = pl.ds(g * wide, wide)
        part = dot(mixed[here, at], w_out[at, :])
        total = part + (encoded[here, :].astype(F32) if g == 0 else acc[here, :])
        if g < GROUPS - 1:
            acc[here, :] = total
        else:
            out_ref[here, :] = total.astype(BF16)

    for g in range(GROUPS):
        values(g)
    end_copy(1, PEERS - 1).wait_recv()
    spread = (iota((heads, lanes_all), 1) // hd == iota((heads, lanes_all), 0)).astype(F32)
    skip_lanes[...] = exact(jnp.broadcast_to(skip_ref[...], (8, heads)), spread)
    gates(0)
    gates(1)
    for top, deep in ((0, half), (half, count)):
        causal = iota((half, deep), 0) + top >= iota((half, deep), 1)
        masked[top : top + half, :deep] = jnp.where(
            causal, dot(c_rows[top : top + half, :], b_t[:, :deep]), 0.0
        ).astype(BF16)
    scan(0)
    gates(2)
    inner(0)
    scan(1)
    gates(3)
    inner(1)
    scan(2)
    inner(2)
    inner(3)
    scan(3)
    loads[6 + GROUPS].wait()
    for g in range(GROUPS):
        all_copies(e_out, e_in, send2, recv2, g).wait_recv()
        pipelined(functools.partial(finish, g), functools.partial(merge, g), blocks)

    end_copy(1, PEERS - 1).wait_send()
    for g in range(GROUPS):
        all_copies(s_out, s_in, send1, recv1, g).wait_send()
        all_copies(e_out, e_in, send2, recv2, g).wait_send()


def body(frames, patch_cell, enc_in, enc_bias, enc_out, pos_table, norm_gain, w_pair, w_keys,
         w_step, step_bias, decay_code, skip_gain, out_gain, w_out):
    count, pixels = frames.shape[0], frames.shape[2]
    depth = enc_out.shape[1]
    heads = w_step.shape[1]
    lanes = w_out.shape[0]
    width = w_keys.shape[1] // 2
    slice_rows = width * lanes // (GROUPS * PEERS * LANES)
    vm = pltpu.VMEM
    comm = vm((GROUPS, PEERS, slice_rows, LANES), BF16)
    dma = pltpu.SemaphoreType.DMA
    out = pl.pallas_call(
        kernel,
        out_shape=jax.ShapeDtypeStruct((count, depth), BF16),
        in_specs=[pl.BlockSpec(memory_space=pl.ANY)] * 8
        + [pl.BlockSpec(memory_space=pltpu.SMEM)]
        + [pl.BlockSpec(memory_space=pltpu.VMEM)] * 6,
        out_specs=pl.BlockSpec(memory_space=pltpu.VMEM),
        scratch_shapes=[
            vm((count, pixels), BF16), vm((pixels, depth), BF16), vm((depth, depth), BF16),
            vm((pos_table.shape[0] // 16, 16, depth), BF16), vm((depth, 2 * width), BF16), vm((heads, depth), BF16),
            vm((depth, 2 * lanes), BF16), vm((lanes, depth), BF16),
            vm((count, depth), BF16), vm((count, depth), F32), vm((count, depth), BF16),
            vm((count, depth), BF16), vm((depth, 128), BF16), vm((count, 128), BF16), vm((width, count), BF16),
            vm((count, width), BF16), vm((count, 128), BF16), vm((count, count), BF16),
            vm((depth, lanes), BF16), vm((depth, lanes), BF16), vm((count, lanes), BF16),
            vm((count, lanes), BF16),
            vm((count, lanes), F32), vm((count, lanes), F32), vm((count, lanes), F32),
            vm((count, depth), F32), vm((count, lanes), BF16), vm((8, lanes), F32),
            vm((8, 128), F32), vm((PEERS, 8, 128), F32), comm, comm, comm, comm,
            dma((7 + GROUPS,)), dma, dma,
            dma((GROUPS,)), dma((GROUPS,)), dma((GROUPS,)), dma((GROUPS,)),
        ],
        compiler_params=pltpu.CompilerParams(
            collective_id=0, has_side_effects=True, vmem_limit_bytes=VMEM_LIMIT
        ),
        name="layer",
    )(
        frames.reshape(count, pixels), enc_in, enc_out,
        pos_table.reshape(pos_table.shape[0] // 16, 16, depth), w_keys, w_step.T, w_pair, w_out,
        patch_cell, enc_bias[None], norm_gain[None], step_bias[None], decay_code[None],
        skip_gain[None], out_gain[None],
    )
    return out[:, None]


def solution(mesh):
    placed = (P("tm", "space", None), P("space")) + (P(),) * 13
    return jax.shard_map(
        body, mesh=mesh, in_specs=placed, out_specs=P("tm", "space", None), check_vma=False
    )
```

time: 130 us -> 31.9 us (0.25)
  local copies, waits for them, and re-layouts: 41.5 us -> 2.26 us
  matrix products: 37 us -> 0 us
  Pallas kernels: 0 us -> 28.8 us
  other arithmetic: 27.4 us -> 0 us
  waiting for transfers between devices: 11.6 us -> 0 us
  starting transfers between devices: 10.9 us -> 0 us
    dot_general x8 -> x0, matrix products: 37 us -> none  [dot(): return jnp.dot(a, b, preferred_element_type=F32)]
    pallas_call x0 -> x1, Pallas kernels: none -> 28.8 us  [body(): pl.pallas_call(kernel, out_shape=jax.ShapeDtypeStruct((count, depth), BF1...]
    convert_element_type x3 -> x0, local copies, waits for them, and re-layouts: 17.3 us -> none  [the longest x1 6.48 us: body(): pair = dot(normed, w_pair).astype(BF16).reshape(count, heads, 2, hd)]
    mul x7 -> x0, local copies, waits for them, and re-layouts: 16 us -> none  [the longest x2 7.94 us: body(): linear.reshape(count, heads, hd) * jnp.exp(cum)[:, :, None]]
    all_to_all x2 -> x0, waiting for transfers between devices: 11.6 us -> none  [the longest x1 11.6 us: body(): lax.all_to_all(outgoing, 'tm', split_axis=0, concat_axis=0, tiled=True)]
    all_to_all x2 -> x0, starting transfers between devices: 10.9 us -> none  [the longest x1 7.14 us: body(): lax.all_to_all(outgoing, 'tm', split_axis=0, concat_axis=0, tiled=True)]
    unnamed x14 -> x0, other arithmetic: 9.88 us -> none
    convert_element_type x3 -> x0, other arithmetic: 9.65 us -> none  [the longest x1 6.84 us: body(): g = y * jax.nn.silu(gate.astype(F32))]
  transfers between devices with their start and end apart: 2 -> 0, of which waited for: 1 -> 0; matrix products, arithmetic and copies ran while one was open for 18% -> 0% of each run, Pallas kernels for 0% -> 0%
where the time goes in v3:
time: 31.9 us; the launch traced here: 31.7 us
  Pallas kernels  28.8 us (90%)
  local copies, waits for them, and re-layouts  2.26 us (7%)
  between operations  0.66 us (2%)
    pallas_call x1, Pallas kernels, body(): pl.pallas_call(kernel, out_shape=jax.ShapeDtypeStruct((count, depth), BF1...  28.8 us
    unnamed x1, local copies, waits for them, and re-layouts  2.26 us

profile of v3, /device:TPU:0, one launch (start us, length us, event | category | flops | bytes accessed | tf_op | source)
XLA Modules:
  0.0 31.7 jit_solution(16025422109224019498)
XLA Ops:
  0.7 28.8 %layer.1 = bf16[512,1024]{1,0:T(8,128)(2,1)} custom-call(bf16[512,256]{1,0:T(8,128)(2,1)} %bitcast.12, bf16[256,1024]{1,0:T(8,128)(2,1)} %enc_in_hbm.1, bf16[1024,1024]{1,0:T(8,128)(2,1)} %enc_out_hbm.1, bf16[128,16,1024]{2,1,0:T(8,128)(2,1)} %bitcast.10, bf16[1024,256]{1,0:T(8,128)(2,1)} %w_keys_hbm.1, bf16[32,1024]{1,0:T(8,128)(2,1)} %bitcast.13, ...), custom_call_target="tpu_custom_call" | custom-call | tf_op jit(solution)/shard_map/layer/pallas_call | solution.py:311
  29.4 2.3 %copy.18 = bf16[512,1,1024]{2,0,1:T(8,128)(2,1)} copy(bf16[512,1,1024]{2,0,1:T(8,128)(2,1)} %bitcast.11) | data formatting | bytes 2097152

commit v4 on v3

v4 whole, which is shorter than its diff:
```python
import functools

import jax
import jax.numpy as jnp
from jax import lax
from jax.experimental import pallas as pl
from jax.experimental.pallas import tpu as pltpu
from jax.sharding import PartitionSpec as P

F32 = jnp.float32
BF16 = jnp.bfloat16
MESH = pl.DeviceIdType.MESH
SIZES = (512, 768, 512, 256)
GROUPS = len(SIZES)
STARTS = tuple(sum(SIZES[:g]) for g in range(GROUPS))
PARTS = 8
PEERS = 16
ROWS = 128
BIG = 256
VMEM_LIMIT = 54 * 1024 * 1024


def dot(a, b):
    return jnp.dot(a, b, preferred_element_type=F32)


def exact(a, b):
    return jnp.dot(a, b, preferred_element_type=F32, precision=lax.Precision.HIGHEST)


def iota(shape, axis):
    return lax.broadcasted_iota(jnp.int32, shape, axis)


def pipelined(first, second, blocks, third=None):
    first(0)
    for n in range(blocks):
        if n + 1 < blocks:
            first(n + 1)
        second(n)
        if third is not None and n > 0:
            third(n - 1)
    if third is not None:
        third(blocks - 1)


def kernel(
    frames_hbm, enc_in_hbm, enc_out_hbm, pos_hbm, w_keys_hbm, w_step_hbm, w_pair_hbm, w_out_hbm,
    cell_ref, enc_bias_ref, norm_gain_ref, step_bias_ref, code_ref, skip_ref, out_gain_ref,
    out_hbm,
    frames, enc_in, enc_out, pos_table, w_keys, w_step, w_pair, w_out,
    hidden, encoded, normed, step_w, step_v, b_t, c_rows, dec, masked,
    w_val, w_gate, x_v, xs_v, sz_v, grow_v, y_v, acc, mixed, skip_lanes,
    out_v, end_out, end_in, *rest,
):
    count, depth = encoded.shape
    heads = step_bias_ref.shape[1]
    width = c_rows.shape[1]
    lanes_all = x_v.shape[1]
    s_out, s_in, e_out, e_in = (rest[k * GROUPS : (k + 1) * GROUPS] for k in range(4))
    load_sem, store_sem, end_send, end_recv, send1, recv1, send2, recv2 = rest[4 * GROUPS :]
    hd = lanes_all // heads
    me = lax.axis_index("tm")

    def pair_part(g):
        part = pl.ds(2 * STARTS[g], 2 * SIZES[g])
        return (w_pair_hbm.at[:, part], w_pair.at[:, part])

    plan = [
        (frames_hbm, frames), (enc_in_hbm, enc_in), (enc_out_hbm, enc_out), (pos_hbm, pos_table),
        (w_keys_hbm, w_keys), (w_step_hbm, w_step),
    ]
    plan += [pair_part(g) for g in range(GROUPS)]
    plan.append((w_out_hbm, w_out))
    loads = [
        pltpu.make_async_copy(src, dst, load_sem.at[n]) for n, (src, dst) in enumerate(plan)
    ]
    for load in loads:
        load.start()

    barrier = pltpu.get_barrier_semaphore()

    def peer_at(d):
        return lax.rem(me + d, PEERS)

    for d in range(1, PEERS):
        pl.semaphore_signal(barrier, inc=1, device_id={"tm": peer_at(d)}, device_id_type=MESH)

    four = (iota((heads, 128), 1) % heads == iota((heads, 128), 0)).astype(F32)
    bias4 = exact(jnp.broadcast_to(step_bias_ref[...], (8, heads)), four)[:1]
    code4 = dot(jnp.broadcast_to(code_ref[...], (8, heads)).astype(BF16), four.astype(BF16))[:1]
    rate4 = (-0.0005 - 0.003 * code4) * 1.4426950408889634
    loads[0].wait()
    loads[1].wait()

    def hide(n):
        at = pl.ds(n * BIG, BIG)
        raw = dot(frames[at, :], enc_in[...]) + enc_bias_ref[...]
        near = 0.5 * raw
        bent = jnp.tanh(raw * (0.7978845608028654 + 0.035677408136300125 * (raw * raw)))
        hidden[at, :] = (near + near * bent).astype(BF16)

    def draw(n):
        at = pl.ds(n * BIG, BIG)
        acc[at, :] = dot(hidden[at, :], enc_out[...])

    hide(0)
    loads[2].wait()
    pipelined(lambda n: hide(n) if n else None, draw, count // BIG)

    for n in (3, 4, 5, 6):
        loads[n].wait()
    cell = cell_ref[0]
    near = pos_table[lax.div(cell, 16)].astype(F32)
    pos_row = jnp.sum(
        jnp.where(iota((16, depth), 0) == lax.rem(cell, 16), near, 0.0), axis=0, keepdims=True
    )
    step_w[...] = jnp.concatenate([w_step[...]] * (128 // heads), axis=0).T

    def pack(first, last):
        for k in range(first, last):
            v0 = w_pair[:, 256 * k : 256 * k + 128]
            v1 = pltpu.roll(w_pair[:, 256 * k + 128 : 256 * k + 256], hd, 1)
            left = iota((depth, 128), 1) < hd
            w_val[:, 128 * k : 128 * k + 128] = jnp.where(left, v0, v1)
            w_gate[:, 128 * k : 128 * k + 128] = jnp.where(left, v1, v0)

    def code(n):
        at = pl.ds(n * ROWS, ROWS)
        coded = (acc[at, :] + pos_row).astype(BF16)
        encoded[at, :] = coded
        plain = coded.astype(F32)
        mean = jnp.mean(plain * plain, axis=-1, keepdims=True)
        normed[at, :] = (plain * lax.rsqrt(mean + 1e-05) * norm_gain_ref[...]).astype(BF16)

    def key(n):
        at = pl.ds(n * BIG, BIG)
        keys = dot(normed[at, :], w_keys[...]).astype(BF16)
        b_t[:, at] = keys[:, :width].T
        c_rows[at, :] = keys[:, width:]
        step_v[at, :] = jax.nn.sigmoid(dot(normed[at, :], step_w[...]) + bias4).astype(BF16)

    blocks = count // ROWS
    each = BIG // ROWS
    pack(0, SIZES[0] // 128)
    pipelined(lambda n: [code(n * each + k) for k in range(each)], key, count // BIG)

    half = count // 2
    lane = iota((half, 128), 1)
    for top, deep in ((0, half), (half, count)):
        causal = iota((half, deep), 0) + top >= iota((half, deep), 1)
        cum = dot(causal.astype(F32).astype(BF16), step_v[:deep, :]) * rate4
        high = cum.astype(BF16).astype(F32)
        mid = (cum - high).astype(BF16).astype(F32)
        low = cum - high - mid
        part = lane // heads
        dec[top : top + half, :] = jnp.where(
            part == 0, high, jnp.where(part == 1, mid, jnp.where(part == 2, low, 0.0))
        ).astype(BF16)
    end_out[...] = jnp.broadcast_to(jnp.exp2(cum[half - 1 : half]), (8, 128))

    pl.semaphore_wait(barrier, PEERS - 1)

    def end_copy(d, n=None):
        return pltpu.make_async_remote_copy(
            src_ref=end_out if n is None else end_in.at[pl.ds(0, n)],
            dst_ref=end_in.at[me] if n is None else end_in.at[pl.ds(0, n)],
            send_sem=end_send, recv_sem=end_recv, device_id={"tm": peer_at(d)}, device_id_type=MESH,
        )

    def slice_copy(src, dst, send, recv, g, d):
        return pltpu.make_async_remote_copy(
            src_ref=src[g].at[peer_at(d)], dst_ref=dst[g].at[me], send_sem=send.at[g],
            recv_sem=recv.at[g], device_id={"tm": peer_at(d)}, device_id_type=MESH,
        )

    def all_copies(src, dst, send, recv, g):
        every = pl.ds(0, PEERS - 1)
        return pltpu.make_async_remote_copy(
            src_ref=src[g].at[every], dst_ref=dst[g].at[every], send_sem=send.at[g],
            recv_sem=recv.at[g], device_id={"tm": peer_at(1)}, device_id_type=MESH,
        )

    for d in range(1, PEERS):
        end_copy(d).start()
    end_in[pl.ds(me, 1)] = end_out[...][None]

    rows = width // PARTS
    sides = PEERS // PARTS

    def values(g):
        if g + 1 < GROUPS:
            loads[7 + g].wait()
            pack(STARTS[g + 1] // 128, (STARTS[g + 1] + SIZES[g + 1]) // 128)
        base, wide = STARTS[g], SIZES[g]
        at = pl.ds(base, wide)
        row, lane = iota((128, wide), 0), iota((128, wide), 1)
        pick = (row % heads == base // hd + lane // hd) & (row < 3 * heads)
        pick = pick.astype(F32).astype(BF16)
        held[g] = dot(dec[...], pick), dot(normed[...], w_val[:, at])

    def scale(g):
        wide = SIZES[g]
        at = pl.ds(STARTS[g], wide)
        cum, x = held.pop(g)
        grow_v[:, at] = jnp.exp2(cum)
        x_v[:, at] = x.astype(BF16)
        xs_v[:, at] = (x * jnp.exp2(-cum)).astype(BF16)
        state = (dot(b_t[...], xs_v[:, at]) * grow_v[count - 1 : count, at]).astype(BF16)
        for side in range(sides):
            lanes = wide // sides
            s_out[g][pl.ds(side * PARTS, PARTS)] = state[
                :, side * lanes : (side + 1) * lanes
            ].reshape(PARTS, rows, lanes)
        for d in range(1, PEERS):
            slice_copy(s_out, s_in, send1, recv1, g, d).start()

    def gates(g):
        held[g] = dot(normed[...], w_gate[:, pl.ds(STARTS[g], SIZES[g])]).astype(BF16).astype(F32)

    def swish(g):
        z = held.pop(g)
        z = z * jax.nn.sigmoid(z)
        for k in range(SIZES[g] // 128):
            sz_v[:, pl.ds(STARTS[g] + 128 * k, 128)] = pltpu.roll(z[:, 128 * k : 128 * k + 128], hd, 1)

    def inner(g):
        at = pl.ds(STARTS[g], SIZES[g])
        for n in range(count // BIG):
            here = pl.ds(n * BIG, BIG)
            deep = (n + 1) * BIG
            sums = dot(masked[here, :deep], xs_v[:deep, at])
            y_v[here, at] = sums * grow_v[here, at] + skip_lanes[0:1, at] * x_v[here, at].astype(F32)

    def scan(g):
        lanes = SIZES[g] // sides
        first = STARTS[g] // hd + (me // PARTS) * (lanes // hd)
        pick = (iota((128, lanes), 0) == first + iota((128, lanes), 1) // hd).astype(F32)
        decay = exact(end_in[:, 0, :], pick)
        all_copies(s_out, s_in, send1, recv1, g).wait_recv()
        s_in[g][pl.ds(me, 1)] = s_out[g][pl.ds(me, 1)]
        running = jnp.zeros((rows, lanes), F32)
        for k in range(PEERS):
            e_out[g][k] = running.astype(BF16)
            if k < PEERS - 1:
                running = decay[k : k + 1] * running + s_in[g][k].astype(F32)
        for d in range(1, PEERS):
            slice_copy(e_out, e_in, send2, recv2, g, d).start()
        e_in[g][pl.ds(me, 1)] = e_out[g][pl.ds(me, 1)]

    square = 256
    mean_of = jnp.where(
        iota((square, square), 0) // hd == iota((square, square), 1) // hd, 1.0 / hd, 0.0
    ).astype(BF16)

    def merge(g, here, cols):
        at = pl.ds(STARTS[g], SIZES[g])
        part = dot(mixed[here, at], w_out[at, cols])
        total = part + (encoded[here, cols].astype(F32) if g == 0 else acc[here, cols])
        if g < GROUPS - 1:
            acc[here, cols] = total
        else:
            out_v[here, cols] = total.astype(BF16)

    def finish(g):
        every, middle = pl.ds(0, count), depth // 2
        wide = SIZES[g]
        state = jnp.concatenate(
            [e_in[g][pl.ds(side * PARTS, PARTS)].reshape(width, wide // sides) for side in range(sides)],
            axis=1,
        )
        carried = dot(c_rows[...], state)
        if g:
            merge(g - 1, every, pl.ds(0, middle))
        means = []
        for k in range(0, wide, square):
            at = pl.ds(STARTS[g] + k, square)
            gated = (y_v[:, at] + grow_v[:, at] * carried[:, k : k + square]) * sz_v[:, at]
            y_v[:, at] = gated
            means.append(dot((gated * gated).astype(BF16), mean_of))
        if g:
            merge(g - 1, every, pl.ds(middle, middle))
        for k in range(0, wide, square):
            at = pl.ds(STARTS[g] + k, square)
            root = lax.rsqrt(means[k // square] + 1e-05)
            mixed[:, at] = (y_v[:, at] * root * out_gain_ref[:, at]).astype(BF16)

    held = {}
    for g in range(GROUPS):
        values(g)
        scale(g)
    end_copy(1, PEERS - 1).wait_recv()
    spread = (iota((heads, lanes_all), 1) // hd == iota((heads, lanes_all), 0)).astype(F32)
    skip_lanes[...] = exact(jnp.broadcast_to(skip_ref[...], (8, heads)), spread)
    def mask(n):
        here, deep = pl.ds(n * BIG, BIG), (n + 1) * BIG
        causal = iota((BIG, deep), 0) + n * BIG >= iota((BIG, deep), 1)
        masked[here, :deep] = jnp.where(causal, dot(c_rows[here, :], b_t[:, :deep]), 0.0).astype(BF16)

    gates(0)
    gates(1)
    swish(0)
    for n in range(count // BIG):
        mask(n)
    swish(1)
    scan(0)
    gates(2)
    inner(0)
    swish(2)
    scan(1)
    gates(3)
    inner(1)
    swish(3)
    scan(2)
    inner(2)
    inner(3)
    scan(3)
    loads[6 + GROUPS].wait()
    for g in range(GROUPS):
        all_copies(e_out, e_in, send2, recv2, g).wait_recv()
        finish(g)

    def store(n):
        here = pl.ds(n * ROWS, ROWS)
        return pltpu.make_async_copy(out_v.at[here], out_hbm.at[here], store_sem.at[n])

    for n in range(blocks):
        merge(GROUPS - 1, pl.ds(n * ROWS, ROWS), pl.ds(0, depth))
        store(n).start()

    end_copy(1, PEERS - 1).wait_send()
    for g in range(GROUPS):
        all_copies(s_out, s_in, send1, recv1, g).wait_send()
        all_copies(e_out, e_in, send2, recv2, g).wait_send()

    for n in range(blocks):
        store(n).wait()


def body(frames, patch_cell, enc_in, enc_bias, enc_out, pos_table, norm_gain, w_pair, w_keys,
         w_step, step_bias, decay_code, skip_gain, out_gain, w_out):
    count, pixels = frames.shape[0], frames.shape[2]
    depth = enc_out.shape[1]
    heads = w_step.shape[1]
    lanes = w_out.shape[0]
    width = w_keys.shape[1] // 2
    vm = pltpu.VMEM
    comm = [vm((PEERS, width // PARTS, wide * PARTS // PEERS), BF16) for wide in SIZES]
    dma = pltpu.SemaphoreType.DMA
    out = pl.pallas_call(
        kernel,
        out_shape=jax.ShapeDtypeStruct((count, depth), BF16),
        in_specs=[pl.BlockSpec(memory_space=pltpu.HBM)] * 8
        + [pl.BlockSpec(memory_space=pltpu.SMEM)]
        + [pl.BlockSpec(memory_space=pltpu.VMEM)] * 6,
        out_specs=pl.BlockSpec(memory_space=pl.ANY),
        scratch_shapes=[
            vm((count, pixels), BF16), vm((pixels, depth), BF16), vm((depth, depth), BF16),
            vm((pos_table.shape[0] // 16, 16, depth), BF16), vm((depth, 2 * width), BF16), vm((heads, depth), BF16),
            vm((depth, 2 * lanes), BF16), vm((lanes, depth), BF16),
            vm((count, depth), BF16), vm((count, depth), BF16),
            vm((count, depth), BF16), vm((depth, 128), BF16), vm((count, 128), BF16), vm((width, count), BF16),
            vm((count, width), BF16), vm((count, 128), BF16), vm((count, count), BF16),
            vm((depth, lanes), BF16), vm((depth, lanes), BF16), vm((count, lanes), BF16),
            vm((count, lanes), BF16),
            vm((count, lanes), F32), vm((count, lanes), F32), vm((count, lanes), F32),
            vm((count, depth), F32), vm((count, lanes), BF16), vm((8, lanes), F32),
            vm((count, depth), BF16), vm((8, 128), F32), vm((PEERS, 8, 128), F32), *comm * 4,
            dma((7 + GROUPS,)), dma((count // ROWS,)), dma, dma,
            dma((GROUPS,)), dma((GROUPS,)), dma((GROUPS,)), dma((GROUPS,)),
        ],
        compiler_params=pltpu.CompilerParams(
            collective_id=0, has_side_effects=True, vmem_limit_bytes=VMEM_LIMIT
        ),
        name="layer",
    )(
        frames.reshape(count, pixels), enc_in, enc_out,
        pos_table.reshape(pos_table.shape[0] // 16, 16, depth), w_keys, w_step.T, w_pair, w_out,
        patch_cell, enc_bias[None], norm_gain[None], step_bias[None], decay_code[None],
        skip_gain[None], out_gain[None],
    )
    return out[:, None]


def solution(mesh):
    placed = (P("tm", "space", None), P("space")) + (P(),) * 13
    return jax.shard_map(
        body, mesh=mesh, in_specs=placed, out_specs=P("tm", "space", None), check_vma=False
    )
```

time: 31.9 us -> 32.9 us (1.031)
  Pallas kernels: 28.8 us -> 29.7 us
    pallas_call x1, Pallas kernels: 28.8 us -> 29.7 us  [body(): pl.pallas_call(kernel, out_shape=jax.ShapeDtypeStruct((count, depth), BF1...]
where the time goes in v4:
time: 32.9 us; the launch traced here: 32.7 us
  Pallas kernels  29.7 us (90%)
  local copies, waits for them, and re-layouts  2.26 us (7%)
  between operations  0.66 us (2%)
    pallas_call x1, Pallas kernels, body(): pl.pallas_call(kernel, out_shape=jax.ShapeDtypeStruct((count, depth), BF1...  29.7 us
    unnamed x1, local copies, waits for them, and re-layouts  2.26 us

profile of v4, /device:TPU:0, one launch (start us, length us, event | category | flops | bytes accessed | tf_op | source)
XLA Modules:
  0.0 32.7 jit_solution(4981945250676696948)
XLA Ops:
  0.7 29.7 %layer.1 = bf16[512,1024]{1,0:T(8,128)(2,1)} custom-call(bf16[512,256]{1,0:T(8,128)(2,1)} %bitcast.12, bf16[256,1024]{1,0:T(8,128)(2,1)} %enc_in_hbm.1, bf16[1024,1024]{1,0:T(8,128)(2,1)} %enc_out_hbm.1, bf16[128,16,1024]{2,1,0:T(8,128)(2,1)} %bitcast.10, bf16[1024,256]{1,0:T(8,128)(2,1)} %w_keys_hbm.1, bf16[32,1024]{1,0:T(8,128)(2,1)} %bitcast.13, ...), custom_call_target="tpu_custom_call" | custom-call | tf_op jit(solution)/shard_map/layer/pallas_call | solution.py:350
  30.4 2.3 %copy.18 = bf16[512,1,1024]{2,0,1:T(8,128)(2,1)} copy(bf16[512,1,1024]{2,0,1:T(8,128)(2,1)} %bitcast.11) | data formatting | bytes 2097152

commit v5 on v3

--- a/solution.py
+++ b/solution.py
@@ -13,8 +13,9 @@
 GROUPS = 4
 LANES = 256
 PEERS = 16
-ROWS = 128
-VMEM_LIMIT = 60 * 1024 * 1024
+ROWS = 256
+BIG = 256
+VMEM_LIMIT = 54 * 1024 * 1024
 
 
 def dot(a, b):
@@ -44,12 +45,12 @@
 def kernel(
     frames_hbm, enc_in_hbm, enc_out_hbm, pos_hbm, w_keys_hbm, w_step_hbm, w_pair_hbm, w_out_hbm,
     cell_ref, enc_bias_ref, norm_gain_ref, step_bias_ref, code_ref, skip_ref, out_gain_ref,
-    out_ref,
+    out_hbm,
     frames, enc_in, enc_out, pos_table, w_keys, w_step, w_pair, w_out,
-    hidden, raw, encoded, normed, step_w, step_v, b_t, c_rows, dec, masked,
+    hidden, encoded, normed, step_w, step_v, b_t, c_rows, dec, masked,
     w_val, w_gate, x_v, xs_v, sz_v, grow_v, y_v, acc, mixed, skip_lanes,
-    end_out, end_in, s_out, s_in, e_out, e_in,
-    load_sem, end_send, end_recv, send1, recv1, send2, recv2,
+    out_v, end_out, end_in, s_out, s_in, e_out, e_in,
+    load_sem, store_sem, end_send, end_recv, send1, recv1, send2, recv2,
 ):
     count, depth = encoded.shape
     heads = step_bias_ref.shape[1]
@@ -86,27 +87,24 @@
     four = (iota((heads, 128), 1) % heads == iota((heads, 128), 0)).astype(F32)
     bias4 = exact(jnp.broadcast_to(step_bias_ref[...], (8, heads)), four)[:1]
     code4 = dot(jnp.broadcast_to(code_ref[...], (8, heads)).astype(BF16), four.astype(BF16))[:1]
-    rate4 = -0.0005 - 0.003 * code4
+    rate4 = (-0.0005 - 0.003 * code4) * 1.4426950408889634
     loads[0].wait()
     loads[1].wait()
 
     def hide(n):
-        at = pl.ds(n * ROWS, ROWS)
+        at = pl.ds(n * BIG, BIG)
         raw = dot(frames[at, :], enc_in[...]) + enc_bias_ref[...]
-        hidden[at, :] = jax.nn.gelu(raw, approximate=True).astype(BF16)
+        near = 0.5 * raw
+        bent = jnp.tanh(raw * (0.7978845608028654 + 0.035677408136300125 * (raw * raw)))
+        hidden[at, :] = (near + near * bent).astype(BF16)
 
     def draw(n):
-        at = pl.ds(n * ROWS, ROWS)
-        raw[at, :] = dot(hidden[at, :], enc_out[...])
-
-    blocks = count // ROWS
+        at = pl.ds(n * BIG, BIG)
+        acc[at, :] = dot(hidden[at, :], enc_out[...])
+
     hide(0)
-    hide(1)
     loads[2].wait()
-    for n in range(blocks):
-        draw(n)
-        if n + 2 < blocks:
-            hide(n + 2)
+    pipelined(lambda n: hide(n) if n else None, draw, count // BIG)
 
     for n in (3, 4, 5, 6):
         loads[n].wait()
@@ -117,8 +115,8 @@
     )
     step_w[...] = jnp.concatenate([w_step[...]] * (128 // heads), axis=0).T
 
-    def pack(g):
-        for k in range(g * (wide // 128), (g + 1) * (wide // 128)):
+    def pack(first, last):
+        for k in range(first, last):
             v0 = w_pair[:, 256 * k : 256 * k + 128]
             v1 = pltpu.roll(w_pair[:, 256 * k + 128 : 256 * k + 256], hd, 1)
             left = iota((depth, 128), 1) < hd
@@ -127,21 +125,23 @@
 
     def code(n):
         at = pl.ds(n * ROWS, ROWS)
-        coded = (raw[at, :] + pos_row).astype(BF16)
+        coded = (acc[at, :] + pos_row).astype(BF16)
         encoded[at, :] = coded
         plain = coded.astype(F32)
         mean = jnp.mean(plain * plain, axis=-1, keepdims=True)
         normed[at, :] = (plain * lax.rsqrt(mean + 1e-05) * norm_gain_ref[...]).astype(BF16)
 
     def key(n):
-        at = pl.ds(n * ROWS, ROWS)
+        at = pl.ds(n * BIG, BIG)
         keys = dot(normed[at, :], w_keys[...]).astype(BF16)
         b_t[:, at] = keys[:, :width].T
         c_rows[at, :] = keys[:, width:]
         step_v[at, :] = jax.nn.sigmoid(dot(normed[at, :], step_w[...]) + bias4).astype(BF16)
 
-    pipelined(code, key, blocks)
-    pack(0)
+    blocks = count // ROWS
+    each = BIG // ROWS
+    pack(0, wide // 128)
+    pipelined(lambda n: [code(n * each + k) for k in range(each)], key, count // BIG)
 
     half = count // 2
     lane = iota((half, 128), 1)
@@ -155,7 +155,7 @@
         dec[top : top + half, :] = jnp.where(
             part == 0, high, jnp.where(part == 1, mid, jnp.where(part == 2, low, 0.0))
         ).astype(BF16)
-    end_out[...] = jnp.broadcast_to(jnp.exp(cum[half - 1 : half]), (8, 128))
+    end_out[...] = jnp.broadcast_to(jnp.exp2(cum[half - 1 : half]), (8, 128))
 
     pl.semaphore_wait(barrier, PEERS - 1)
 
@@ -190,40 +190,43 @@
     def values(g):
         if g + 1 < GROUPS:
             loads[7 + g].wait()
+            pack((g + 1) * (wide // 128), (g + 2) * (wide // 128))
         at = pl.ds(g * wide, wide)
-        x = dot(normed[...], w_val[:, at]).astype(BF16)
-        x_v[:, at] = x
         row, lane = iota((128, wide), 0), iota((128, wide), 1)
         pick = (row % heads == g * (wide // hd) + lane // hd) & (row < 3 * heads)
-        cum = dot(dec[...], pick.astype(F32).astype(BF16))
-        grow = jnp.exp(cum)
-        grow_v[:, at] = grow
-        scaled = (x.astype(F32) * jnp.exp(-cum)).astype(BF16)
-        xs_v[:, at] = scaled
-        state = (dot(b_t[...], scaled) * grow[count - 1 : count]).astype(BF16)
+        pick = pick.astype(F32).astype(BF16)
+        held[g] = dot(dec[...], pick), dot(normed[...], w_val[:, at])
+
+    def scale(g):
+        at = pl.ds(g * wide, wide)
+        cum, x = held.pop(g)
+        grow_v[:, at] = jnp.exp2(cum)
+        x_v[:, at] = x.astype(BF16)
+        xs_v[:, at] = (x * jnp.exp2(-cum)).astype(BF16)
+        state = (dot(b_t[...], xs_v[:, at]) * grow_v[count - 1 : count, at]).astype(BF16)
         for side in range(sides):
             s_out[g, pl.ds(side * parts, parts)] = state[
                 :, side * LANES : (side + 1) * LANES
             ].reshape(parts, rows, LANES)
-        if g + 1 < GROUPS:
-            pack(g + 1)
         for d in range(1, PEERS):
             slice_copy(s_out, s_in, send1, recv1, g, d).start()
 
     def gates(g):
-        at = pl.ds(g * wide, wide)
-        z = dot(normed[...], w_gate[:, at]).astype(BF16).astype(F32)
+        held[g] = dot(normed[...], w_gate[:, pl.ds(g * wide, wide)]).astype(BF16).astype(F32)
+
+    def swish(g):
+        z = held.pop(g)
         z = z * jax.nn.sigmoid(z)
         for k in range(wide // 128):
             sz_v[:, pl.ds(g * wide + 128 * k, 128)] = pltpu.roll(z[:, 128 * k : 128 * k + 128], hd, 1)
 
     def inner(g):
         at = pl.ds(g * wide, wide)
-        base = skip_lanes[0:1, at]
-        for top, deep in ((0, half), (half, count)):
-            here = pl.ds(top, half)
+        for n in range(count // BIG):
+            here = pl.ds(n * BIG, BIG)
+            deep = (n + 1) * BIG
             sums = dot(masked[here, :deep], xs_v[:deep, at])
-            y_v[here, at] = sums * grow_v[here, at] + base * x_v[here, at].astype(F32)
+            y_v[here, at] = sums * grow_v[here, at] + skip_lanes[0:1, at] * x_v[here, at].astype(F32)
 
     def scan(g):
         first = (g * sides + me // parts) * (LANES // hd)
@@ -254,6 +257,10 @@
             mean = dot((gated * gated).astype(BF16), mean_of)
             mixed[here, at] = (gated * lax.rsqrt(mean + 1e-05) * out_gain_ref[:, at]).astype(BF16)
 
+    def store(n):
+        here = pl.ds(n * ROWS, ROWS)
+        return pltpu.make_async_copy(out_v.at[here], out_hbm.at[here], store_sem.at[n])
+
     def merge(g, n):
         here = pl.ds(n * ROWS, ROWS)
         at = pl.ds(g * wide, wide)
@@ -262,27 +269,36 @@
         if g < GROUPS - 1:
             acc[here, :] = total
         else:
-            out_ref[here, :] = total.astype(BF16)
-
+            out_v[here, :] = total.astype(BF16)
+            store(n).start()
+
+    held = {}
     for g in range(GROUPS):
         values(g)
+        scale(g)
     end_copy(1, PEERS - 1).wait_recv()
     spread = (iota((heads, lanes_all), 1) // hd == iota((heads, lanes_all), 0)).astype(F32)
     skip_lanes[...] = exact(jnp.broadcast_to(skip_ref[...], (8, heads)), spread)
+    def mask(n):
+        here, deep = pl.ds(n * BIG, BIG), (n + 1) * BIG
+        causal = iota((BIG, deep), 0) + n * BIG >= iota((BIG, deep), 1)
+        masked[here, :deep] = jnp.where(causal, dot(c_rows[here, :], b_t[:, :deep]), 0.0).astype(BF16)
+
     gates(0)
     gates(1)
-    for top, deep in ((0, half), (half, count)):
-        causal = iota((half, deep), 0) + top >= iota((half, deep), 1)
-        masked[top : top + half, :deep] = jnp.where(
-            causal, dot(c_rows[top : top + half, :], b_t[:, :deep]), 0.0
-        ).astype(BF16)
+    swish(0)
+    swish(1)
     scan(0)
     gates(2)
-    inner(0)
+    for n in range(count // BIG):
+        mask(n)
+    swish(2)
     scan(1)
     gates(3)
+    inner(0)
+    swish(3)
+    scan(2)
     inner(1)
-    scan(2)
     inner(2)
     inner(3)
     scan(3)
@@ -295,6 +311,9 @@
     for g in range(GROUPS):
         all_copies(s_out, s_in, send1, recv1, g).wait_send()
         all_copies(e_out, e_in, send2, recv2, g).wait_send()
+
+    for n in range(blocks):
+        store(n).wait()
 
 
 def body(frames, patch_cell, enc_in, enc_bias, enc_out, pos_table, norm_gain, w_pair, w_keys,
@@ -311,23 +330,23 @@
     out = pl.pallas_call(
         kernel,
         out_shape=jax.ShapeDtypeStruct((count, depth), BF16),
-        in_specs=[pl.BlockSpec(memory_space=pl.ANY)] * 8
+        in_specs=[pl.BlockSpec(memory_space=pltpu.HBM)] * 8
         + [pl.BlockSpec(memory_space=pltpu.SMEM)]
         + [pl.BlockSpec(memory_space=pltpu.VMEM)] * 6,
-        out_specs=pl.BlockSpec(memory_space=pltpu.VMEM),
+        out_specs=pl.BlockSpec(memory_space=pl.ANY),
         scratch_shapes=[
             vm((count, pixels), BF16), vm((pixels, depth), BF16), vm((depth, depth), BF16),
             vm((pos_table.shape[0] // 16, 16, depth), BF16), vm((depth, 2 * width), BF16), vm((heads, depth), BF16),
             vm((depth, 2 * lanes), BF16), vm((lanes, depth), BF16),
-            vm((count, depth), BF16), vm((count, depth), F32), vm((count, depth), BF16),
+            vm((count, depth), BF16), vm((count, depth), BF16),
             vm((count, depth), BF16), vm((depth, 128), BF16), vm((count, 128), BF16), vm((width, count), BF16),
             vm((count, width), BF16), vm((count, 128), BF16), vm((count, count), BF16),
             vm((depth, lanes), BF16), vm((depth, lanes), BF16), vm((count, lanes), BF16),
             vm((count, lanes), BF16),
             vm((count, lanes), F32), vm((count, lanes), F32), vm((count, lanes), F32),
             vm((count, depth), F32), vm((count, lanes), BF16), vm((8, lanes), F32),
-            vm((8, 128), F32), vm((PEERS, 8, 128), F32), comm, comm, comm, comm,
-            dma((7 + GROUPS,)), dma, dma,
+            vm((count, depth), BF16), vm((8, 128), F32), vm((PEERS, 8, 128), F32), comm, comm, comm, comm,
+            dma((7 + GROUPS,)), dma((count // ROWS,)), dma, dma,
             dma((GROUPS,)), dma((GROUPS,)), dma((GROUPS,)), dma((GROUPS,)),
         ],
         compiler_params=pltpu.CompilerParams(

time: 31.9 us -> 31.2 us (0.978)
  Pallas kernels: 28.8 us -> 28 us
    pallas_call x1, Pallas kernels: 28.8 us -> 28 us  [body(): pl.pallas_call(kernel, out_shape=jax.ShapeDtypeStruct((count, depth), BF1...]
where the time goes in v5:
time: 31.2 us; the launch traced here: 30.9 us
  Pallas kernels  28 us (90%)
  local copies, waits for them, and re-layouts  2.26 us (7%)
  between operations  0.66 us (2%)
    pallas_call x1, Pallas kernels, body(): pl.pallas_call(kernel, out_shape=jax.ShapeDtypeStruct((count, depth), BF1...  28 us
    unnamed x1, local copies, waits for them, and re-layouts  2.26 us

profile of v5, /device:TPU:0, one launch (start us, length us, event | category | flops | bytes accessed | tf_op | source)
XLA Modules:
  0.0 30.9 jit_solution(11530049646135427858)
XLA Ops:
  0.7 28.0 %layer.1 = bf16[512,1024]{1,0:T(8,128)(2,1)} custom-call(bf16[512,256]{1,0:T(8,128)(2,1)} %bitcast.12, bf16[256,1024]{1,0:T(8,128)(2,1)} %enc_in_hbm.1, bf16[1024,1024]{1,0:T(8,128)(2,1)} %enc_out_hbm.1, bf16[128,16,1024]{2,1,0:T(8,128)(2,1)} %bitcast.10, bf16[1024,256]{1,0:T(8,128)(2,1)} %w_keys_hbm.1, bf16[32,1024]{1,0:T(8,128)(2,1)} %bitcast.13, ...), custom_call_target="tpu_custom_call" | custom-call | tf_op jit(solution)/shard_map/layer/pallas_call | solution.py:330
  28.7 2.3 %copy.18 = bf16[512,1,1024]{2,0,1:T(8,128)(2,1)} copy(bf16[512,1,1024]{2,0,1:T(8,128)(2,1)} %bitcast.11) | data formatting | bytes 2097152

commit v6 on v5

--- a/solution.py
+++ b/solution.py
@@ -13,6 +13,14 @@
 GROUPS = 4
 LANES = 256
 PEERS = 16
+SIDE = 4
+
+
+def hops(step):
+    return sum(min(d, SIDE - d) for d in step)
+
+
+ROUTES = sorted(((n // SIDE, n % SIDE) for n in range(1, PEERS)), key=lambda s: (-hops(s), s))
 ROWS = 256
 BIG = 256
 VMEM_LIMIT = 54 * 1024 * 1024
@@ -79,7 +87,8 @@
     barrier = pltpu.get_barrier_semaphore()
 
     def peer_at(d):
-        return lax.rem(me + d, PEERS)
+        dx, dy = ROUTES[d - 1]
+        return lax.rem(lax.div(me, SIDE) + dx, SIDE) * SIDE + lax.rem(lax.rem(me, SIDE) + dy, SIDE)
 
     for d in range(1, PEERS):
         pl.semaphore_signal(barrier, inc=1, device_id={"tm": peer_at(d)}, device_id_type=MESH)

time: 31.2 us -> 30.8 us (0.987)
    pallas_call x1, Pallas kernels: 28 us -> 27.7 us  [body(): pl.pallas_call(kernel, out_shape=jax.ShapeDtypeStruct((count, depth), BF1...]
where the time goes in v6:
time: 30.8 us; the launch traced here: 30.6 us
  Pallas kernels  27.7 us (90%)
  local copies, waits for them, and re-layouts  2.26 us (7%)
  between operations  0.66 us (2%)
    pallas_call x1, Pallas kernels, body(): pl.pallas_call(kernel, out_shape=jax.ShapeDtypeStruct((count, depth), BF1...  27.7 us
    unnamed x1, local copies, waits for them, and re-layouts  2.26 us

profile of v6, /device:TPU:0, one launch (start us, length us, event | category | flops | bytes accessed | tf_op | source)
XLA Modules:
  0.0 30.6 jit_solution(13605448788726366513)
XLA Ops:
  0.7 27.7 %layer.1 = bf16[512,1024]{1,0:T(8,128)(2,1)} custom-call(bf16[512,256]{1,0:T(8,128)(2,1)} %bitcast.12, bf16[256,1024]{1,0:T(8,128)(2,1)} %enc_in_hbm.1, bf16[1024,1024]{1,0:T(8,128)(2,1)} %enc_out_hbm.1, bf16[128,16,1024]{2,1,0:T(8,128)(2,1)} %bitcast.10, bf16[1024,256]{1,0:T(8,128)(2,1)} %w_keys_hbm.1, bf16[32,1024]{1,0:T(8,128)(2,1)} %bitcast.13, ...), custom_call_target="tpu_custom_call" | custom-call | tf_op jit(solution)/shard_map/layer/pallas_call | solution.py:339
  28.3 2.3 %copy.18 = bf16[512,1,1024]{2,0,1:T(8,128)(2,1)} copy(bf16[512,1,1024]{2,0,1:T(8,128)(2,1)} %bitcast.11) | data formatting | bytes 2097152

commit v7 on v6

--- a/solution.py
+++ b/solution.py
@@ -97,6 +97,8 @@
     bias4 = exact(jnp.broadcast_to(step_bias_ref[...], (8, heads)), four)[:1]
     code4 = dot(jnp.broadcast_to(code_ref[...], (8, heads)).astype(BF16), four.astype(BF16))[:1]
     rate4 = (-0.0005 - 0.003 * code4) * 1.4426950408889634
+    spread = (iota((heads, lanes_all), 1) // hd == iota((heads, lanes_all), 0)).astype(F32)
+    skip_lanes[...] = exact(jnp.broadcast_to(skip_ref[...], (8, heads)), spread)
     loads[0].wait()
     loads[1].wait()
 
@@ -286,8 +288,6 @@
         values(g)
         scale(g)
     end_copy(1, PEERS - 1).wait_recv()
-    spread = (iota((heads, lanes_all), 1) // hd == iota((heads, lanes_all), 0)).astype(F32)
-    skip_lanes[...] = exact(jnp.broadcast_to(skip_ref[...], (8, heads)), spread)
     def mask(n):
         here, deep = pl.ds(n * BIG, BIG), (n + 1) * BIG
         causal = iota((BIG, deep), 0) + n * BIG >= iota((BIG, deep), 1)

time: 30.8 us -> 30.7 us (level)
  no operation moved by 1% of the time
where the time goes in v7:
time: 30.7 us; the launch traced here: 30.5 us
  Pallas kernels  27.6 us (90%)
  local copies, waits for them, and re-layouts  2.26 us (7%)
  between operations  0.66 us (2%)
    pallas_call x1, Pallas kernels, body(): pl.pallas_call(kernel, out_shape=jax.ShapeDtypeStruct((count, depth), BF1...  27.6 us
    unnamed x1, local copies, waits for them, and re-layouts  2.26 us

profile of v7, /device:TPU:0, one launch (start us, length us, event | category | flops | bytes accessed | tf_op | source)
XLA Modules:
  0.0 30.5 jit_solution(17580794057347127193)
XLA Ops:
  0.7 27.6 %layer.1 = bf16[512,1024]{1,0:T(8,128)(2,1)} custom-call(bf16[512,256]{1,0:T(8,128)(2,1)} %bitcast.12, bf16[256,1024]{1,0:T(8,128)(2,1)} %enc_in_hbm.1, bf16[1024,1024]{1,0:T(8,128)(2,1)} %enc_out_hbm.1, bf16[128,16,1024]{2,1,0:T(8,128)(2,1)} %bitcast.10, bf16[1024,256]{1,0:T(8,128)(2,1)} %w_keys_hbm.1, bf16[32,1024]{1,0:T(8,128)(2,1)} %bitcast.13, ...), custom_call_target="tpu_custom_call" | custom-call | tf_op jit(solution)/shard_map/layer/pallas_call | solution.py:339
  28.2 2.3 %copy.18 = bf16[512,1,1024]{2,0,1:T(8,128)(2,1)} copy(bf16[512,1,1024]{2,0,1:T(8,128)(2,1)} %bitcast.11) | data formatting | bytes 2097152
